TPU v7x, 128 devices: a whole 4x4x4 slice. The times are simulated.
128 devices in a mesh: inner: 16 (over x_lo, z, core), outer: 8 (over x_hi, y).
Axes of the slice: x: 4 (x_hi: 2, x_lo: 2; x = x_hi * 2 + x_lo), y: 4, z: 4, core: 2. Of those that a mesh axis runs over, the one named last changes fastest.
Arguments:
- layer_input: bfloat16 [16384, 6144], P(('inner', 'outer')), may hold values from -0.25 to 0.25
- queries: bfloat16 [16384, 768], P(('inner', 'outer')), may hold values from -6 to 6
- keys_values: bfloat16 [16384, 256], P(('inner', 'outer')), may hold values from -6 to 6
- attn_out: bfloat16 [16384, 768], P(('inner', 'outer')), may hold values from -6 to 6
- out_grad: bfloat16 [16384, 768], P(('inner', 'outer')), may hold values from -6 to 6
- log_sums: float32 [6, 16384], P(None, ('inner', 'outer')), may hold values from 5 to 8
- doc_ids: int32 [16384], replicated, may hold values from 0 to 15, never falling along the last dimension, each value on 1 to 2048 neighbouring positions
- span_order: int32 [256], replicated, may hold values from 0 to 255, each once
Outputs:
- query_grad: bfloat16 [16384, 768], P(('inner', 'outer'))
- kv_grad: bfloat16 [16384, 256], P(('inner', 'outer'))
- weight_grad: float32 [6144, 256], P(('inner', 'outer'))
Inputs may be any that keep to these rules, and one draw needn't show every extreme that they name: `doc_ids`: never falling; each document holds 1 to 2048 positions. `span_order`: each span number once.
All inputs are finite; a program needn't handle non-finite values.
Results may differ from a plain program's by a relative error of at most 0.015.
Values may be sent and summed in bfloat16 or wider, within the bound.
A program may use at most 64 MiB of HBM per device.

v0:
```python
import jax
import jax.numpy as jnp
from jax import lax
from jax.sharding import PartitionSpec as P


def passed_along(value, axis, by):
    devices = lax.axis_size(axis)
    return lax.ppermute(value, axis, [(i, (i + by) % devices) for i in range(devices)])


def per_device(
    layer_input, queries, keys_values, attn_out, out_grad, log_sums, doc_ids, span_order
):
    tok_rows = keys_values.shape[0]
    half_len = tok_rows // 2
    head_count = log_sums.shape[0]
    head_dim = keys_values.shape[1] // 2
    inner_size = lax.axis_size("inner")
    outer_size = lax.axis_size("outer")
    my_index = lax.axis_index(("inner", "outer"))
    score_scale = head_dim ** (-0.5)
    row_ids = jnp.arange(tok_rows, dtype=jnp.int32)
    my_spans = lax.dynamic_slice_in_dim(span_order, 2 * my_index, 2)
    query_pos = (
        jnp.where(row_ids < half_len, my_spans[0], my_spans[1]) * half_len + row_ids % half_len
    )
    query_doc = jnp.take(doc_ids, query_pos)
    query_heads = queries.reshape(tok_rows, head_count, head_dim)
    grad_heads = out_grad.reshape(tok_rows, head_count, head_dim)
    out_heads = attn_out.reshape(tok_rows, head_count, head_dim)
    row_delta = jnp.einsum("ihc,ihc->hi", grad_heads, out_heads, preferred_element_type=jnp.float32)

    def key_meta(base_dev, stride, group_devs):
        key_ids = jnp.arange(group_devs * tok_rows, dtype=jnp.int32)
        owner = base_dev + key_ids // tok_rows * stride
        span_ids = 2 * owner + key_ids % tok_rows // half_len
        key_pos = jnp.take(span_order, span_ids) * half_len + key_ids % half_len
        return (key_pos, jnp.take(doc_ids, key_pos))

    def sweep(key_group, kv_grads, query_acc, key_pos, key_doc):
        group_len = key_group.shape[0]
        block_len = 512

        def one_block(block_idx, state):
            first = block_idx * block_len
            key_blk = lax.dynamic_slice_in_dim(key_group, first, block_len, 0)
            pos_blk = lax.dynamic_slice_in_dim(key_pos, first, block_len, 0)
            doc_blk = lax.dynamic_slice_in_dim(key_doc, first, block_len, 0)
            allowed = (pos_blk[None, :] <= query_pos[:, None]) & (
                doc_blk[None, :] == query_doc[:, None]
            )
            grads_now, query_now = state
            key_rows = key_blk[:, :head_dim]
            value_rows = key_blk[:, head_dim:]
            scores = (
                jnp.einsum("ihc,jc->hij", query_heads, key_rows, preferred_element_type=jnp.float32)
                * score_scale
            )
            probs = jnp.exp(jnp.where(allowed[None], scores - log_sums[:, :, None], -1e30))
            probs_low = probs.astype(jnp.bfloat16)
            prob_grads = jnp.einsum(
                "ihc,jc->hij", grad_heads, value_rows, preferred_element_type=jnp.float32
            )
            score_grads = (score_scale * probs * (prob_grads - row_delta[:, :, None])).astype(
                jnp.bfloat16
            )
            query_now = query_now + jnp.einsum(
                "hij,jc->ihc", score_grads, key_rows, preferred_element_type=jnp.float32
            )
            key_part = jnp.einsum(
                "hij,ihc->jc", score_grads, query_heads, preferred_element_type=jnp.float32
            )
            value_part = jnp.einsum(
                "hij,ihc->jc", probs_low, grad_heads, preferred_element_type=jnp.float32
            )
            updated = lax.dynamic_slice_in_dim(grads_now, first, block_len, 0) + jnp.concatenate(
                [key_part, value_part], axis=1
            )
            grads_now = lax.dynamic_update_slice_in_dim(grads_now, updated, first, 0)
            return (grads_now, query_now)

        return lax.fori_loop(0, group_len // block_len, one_block, (kv_grads, query_acc))

    query_zero = jnp.zeros((tok_rows, head_count, head_dim), jnp.float32)
    key_group = lax.all_gather(keys_values, "outer", axis=0, tiled=True)
    inner_pos = lax.axis_index("inner")

    def hop_inner(hop_idx, state):
        group_now, grads_now, query_now = state
        source = (inner_pos - hop_idx) % inner_size
        key_pos, key_doc = key_meta(source * outer_size, 1, outer_size)
        grads_now, query_now = sweep(group_now, grads_now, query_now, key_pos, key_doc)
        grads_now = passed_along(grads_now.astype(jnp.bfloat16), "inner", 1).astype(grads_now.dtype)
        group_now = passed_along(group_now, "inner", 1)
        return (group_now, grads_now, query_now)

    start = (key_group, jnp.zeros((key_group.shape[0], 2 * head_dim), jnp.float32), query_zero)
    key_group, kv_grads, query_acc = lax.fori_loop(0, inner_size, hop_inner, start)
    kv_total = lax.psum_scatter(
        kv_grads.astype(jnp.bfloat16), "outer", scatter_dimension=0, tiled=True
    )
    query_grad = query_acc.astype(jnp.bfloat16).reshape(tok_rows, head_count * head_dim)
    weight_grad = lax.psum_scatter(
        lax.dot_general(
            layer_input, kv_total, (((0,), (0,)), ((), ())), preferred_element_type=jnp.float32
        ),
        ("inner", "outer"),
        scatter_dimension=0,
        tiled=True,
    )
    return (query_grad, kv_total, weight_grad)


def solution(mesh):
    return jax.shard_map(
        per_device,
        mesh=mesh,
        in_specs=(
            P(("inner", "outer"), None),
            P(("inner", "outer"), None),
            P(("inner", "outer"), None),
            P(("inner", "outer"), None),
            P(("inner", "outer"), None),
            P(None, ("inner", "outer")),
            P(),
            P(),
        ),
        out_specs=(
            P(("inner", "outer"), None),
            P(("inner", "outer"), None),
            P(("inner", "outer"), None),
        ),
        check_vma=False,
    )
```

profile of v0, /device:TPU:0, one launch (start us, length us, event | category | flops | bytes accessed | tf_op | source)
XLA Modules:
  0.0 1488.4 jit_solution(5365712212598533073)
XLA Ops:
  16.5 35.7 %all_gather.3 = bf16[1024,256]{1,0:T(8,128)(2,1)S(1)} all-gather(bf16[128,256]{1,0:T(8,128)(2,1)S(1)} %copy-done.4), channel_id=1, replica_groups=mesh['inner'=16,'outer'=8] {'outer'}, dimensions={0}, use_global_device_ids=true | all-gather | bytes 589824 | tf_op jit(solution)/shard_map/all_gather | solution.py:86
  52.4 691.4 %while.64 = (s32[]{:T(128)}, bf16[1024,256]{1,0:T(8,128)(2,1)S(1)}, f32[1024,256]{0,1:T(8,128)}, f32[128,6,128]{0,2,1:T(8,128)S(1)}, s32[]{:T(128)}, /*index=5*/...) while((s32[]{:T(128)}, bf16[1024,256]{1,0:T(8,128)(2,1)S(1)}, ...), condition=%wide.region_3.4_spmd.clone, body=%wide.region_0.3_spmd.clone.sunk | while | flops 507945216 | bytes 26042736 | solution.py:99
  52.5 6.9 gather_fusion
  67.8 10.4 while.65
  81.1 8.9 collective-permute-done.1
  95.7 6.9 gather_fusion
  111.0 10.4 while.65
  122.3 10.9 collective-permute-done.1
  138.9 6.9 gather_fusion
  154.3 10.4 while.65
  165.5 10.9 collective-permute-done.1
  182.1 6.9 gather_fusion
  197.5 10.4 while.65
  208.7 10.9 collective-permute-done.1
  225.3 6.9 gather_fusion
  240.7 10.4 while.65
  251.9 10.9 collective-permute-done.1
  268.5 6.9 gather_fusion
  283.9 10.4 while.65
  295.1 10.9 collective-permute-done.1
  311.7 6.9 gather_fusion
  327.1 10.4 while.65
  338.3 10.9 collective-permute-done.1
  370.3 10.4 while.65
  381.6 10.9 collective-permute-done.1
  413.5 10.4 while.65
  424.8 10.9 collective-permute-done.1
  456.7 10.4 while.65
  468.0 10.9 collective-permute-done.1
  499.9 10.4 while.65
  511.2 10.9 collective-permute-done.1
  527.8 6.9 gather_fusion
  543.1 10.4 while.65
  554.4 10.9 collective-permute-done.1
  571.0 6.9 gather_fusion
  586.3 10.4 while.65
  597.6 10.9 collective-permute-done.1
  614.2 6.9 gather_fusion
  629.5 10.4 while.65
  640.8 10.9 collective-permute-done.1
  657.4 6.9 gather_fusion
  672.8 10.4 while.65
  684.0 10.9 collective-permute-done.1
  700.6 6.9 gather_fusion
  716.0 10.4 while.65
  727.2 10.9 collective-permute-done.1
  746.1 69.0 %reduce-scatter.5.cloned.1.call-done = bf16[128,256]{1,0:T(8,128)(2,1)} async-done(((bf16[1024,256]{1,0:T(8,128)(2,1)}), bf16[128,256]{1,0:T(8,128)(2,1)}) %reduce-scatter.5.cloned.1.call-update) | async-done | bytes 65552 | tf_op jit(solution)/shard_map/reduce_scatter | solution.py:100
  827.1 654.5 %reduce-scatter.7.cloned.1.call-done = f32[48,256]{1,0:T(8,128)} async-done(((f32[6144,256]{1,0:T(8,128)}), f32[48,256]{1,0:T(8,128)}) %reduce-scatter.7.cloned.1.call-update) | async-done | bytes 49168
  (579 shorter events, 456.2 us)
Async XLA Ops:
  7.2 808.0 %copy-start = (bf16[128,6144]{1,0:T(8,128)(2,1)S(1)}, bf16[128,6144]{1,0:T(8,128)(2,1)}, u32[]{:S(2)}) copy-start(bf16[128,6144]{1,0:T(8,128)(2,1)} %param.12) | copy-start | bytes 4718596
  7.2 45.2 %copy-start.1 = (s32[256]{0:T(256)S(1)}, s32[256]{0:T(256)}, u32[]{:S(2)}) copy-start(s32[256]{0:T(256)} %param.19) | copy-start | bytes 3076
  7.2 45.2 %copy-start.2 = (s32[16384]{0:T(1024)S(1)}, s32[16384]{0:T(1024)}, u32[]{:S(2)}) copy-start(s32[16384]{0:T(1024)} %param.18) | copy-start | bytes 196612
  7.2 9.3 copy-start.4
  7.2 45.2 %copy-start.5 = (f32[6,128]{1,0:T(8,128)S(1)}, f32[6,128]{1,0:T(8,128)}, u32[]{:S(2)}) copy-start(f32[6,128]{1,0:T(8,128)} %param.17) | copy-start | bytes 9220
  7.2 807.9 %reduce-scatter.5.cloned.1.call-start = ((), (), s32[]{:S(2)}) async-start(), calls=%async_computation.2 | async-start | bytes 589824 | tf_op jit(solution)/shard_map/reduce_scatter | solution.py:100
  65.6 2.2 copy-start.3
  79.1 10.9 collective-permute-start.1
  79.1 16.5 %collective-permute-start = (bf16[1024,256]{1,0:T(8,128)(2,1)}, bf16[1024,256]{1,0:T(8,128)(2,1)S(1)}, u32[]{:S(2)}, u32[]{:S(2)}) collective-permute-start(bf16[1024,256]{1,0:T(8,128)(2,1)} %copy.80), channel_id=1, source_target_pairs={{0,8},{8,16},{16,24},{24,32},{32,40},{40,48},{48,56},{56,64},{64,7... | collective-permute-start | bytes 1572872 | tf_op jit(solution)/shard_map/while/body/eval_jaxpr/ppermute | solution.py:9
  108.8 2.2 copy-start.3
  122.3 10.9 collective-permute-start.1
  122.3 16.5 %collective-permute-start = (bf16[1024,256]{1,0:T(8,128)(2,1)}, bf16[1024,256]{1,0:T(8,128)(2,1)S(1)}, u32[]{:S(2)}, u32[]{:S(2)}) collective-permute-start(bf16[1024,256]{1,0:T(8,128)(2,1)} %copy.80), channel_id=1, source_target_pairs={{0,8},{8,16},{16,24},{24,32},{32,40},{40,48},{48,56},{56,64},{64,7... | collective-permute-start | bytes 1572872 | tf_op jit(solution)/shard_map/while/body/eval_jaxpr/ppermute | solution.py:9
  152.0 2.2 copy-start.3
  165.5 10.9 collective-permute-start.1
  165.5 16.5 %collective-permute-start = (bf16[1024,256]{1,0:T(8,128)(2,1)}, bf16[1024,256]{1,0:T(8,128)(2,1)S(1)}, u32[]{:S(2)}, u32[]{:S(2)}) collective-permute-start(bf16[1024,256]{1,0:T(8,128)(2,1)} %copy.80), channel_id=1, source_target_pairs={{0,8},{8,16},{16,24},{24,32},{32,40},{40,48},{48,56},{56,64},{64,7... | collective-permute-start | bytes 1572872 | tf_op jit(solution)/shard_map/while/body/eval_jaxpr/ppermute | solution.py:9
  195.2 2.2 copy-start.3
  208.7 10.9 collective-permute-start.1
  208.7 16.5 %collective-permute-start = (bf16[1024,256]{1,0:T(8,128)(2,1)}, bf16[1024,256]{1,0:T(8,128)(2,1)S(1)}, u32[]{:S(2)}, u32[]{:S(2)}) collective-permute-start(bf16[1024,256]{1,0:T(8,128)(2,1)} %copy.80), channel_id=1, source_target_pairs={{0,8},{8,16},{16,24},{24,32},{32,40},{40,48},{48,56},{56,64},{64,7... | collective-permute-start | bytes 1572872 | tf_op jit(solution)/shard_map/while/body/eval_jaxpr/ppermute | solution.py:9
  238.4 2.2 copy-start.3
  251.9 10.9 collective-permute-start.1
  251.9 16.5 %collective-permute-start = (bf16[1024,256]{1,0:T(8,128)(2,1)}, bf16[1024,256]{1,0:T(8,128)(2,1)S(1)}, u32[]{:S(2)}, u32[]{:S(2)}) collective-permute-start(bf16[1024,256]{1,0:T(8,128)(2,1)} %copy.80), channel_id=1, source_target_pairs={{0,8},{8,16},{16,24},{24,32},{32,40},{40,48},{48,56},{56,64},{64,7... | collective-permute-start | bytes 1572872 | tf_op jit(solution)/shard_map/while/body/eval_jaxpr/ppermute | solution.py:9
  281.6 2.2 copy-start.3
  295.1 10.9 collective-permute-start.1
  295.1 16.5 %collective-permute-start = (bf16[1024,256]{1,0:T(8,128)(2,1)}, bf16[1024,256]{1,0:T(8,128)(2,1)S(1)}, u32[]{:S(2)}, u32[]{:S(2)}) collective-permute-start(bf16[1024,256]{1,0:T(8,128)(2,1)} %copy.80), channel_id=1, source_target_pairs={{0,8},{8,16},{16,24},{24,32},{32,40},{40,48},{48,56},{56,64},{64,7... | collective-permute-start | bytes 1572872 | tf_op jit(solution)/shard_map/while/body/eval_jaxpr/ppermute | solution.py:9
  324.8 2.2 copy-start.3
  338.3 10.9 collective-permute-start.1
  338.3 16.5 %collective-permute-start = (bf16[1024,256]{1,0:T(8,128)(2,1)}, bf16[1024,256]{1,0:T(8,128)(2,1)S(1)}, u32[]{:S(2)}, u32[]{:S(2)}) collective-permute-start(bf16[1024,256]{1,0:T(8,128)(2,1)} %copy.80), channel_id=1, source_target_pairs={{0,8},{8,16},{16,24},{24,32},{32,40},{40,48},{48,56},{56,64},{64,7... | collective-permute-start | bytes 1572872 | tf_op jit(solution)/shard_map/while/body/eval_jaxpr/ppermute | solution.py:9
  368.0 2.2 copy-start.3
  381.5 10.9 collective-permute-start.1
  381.6 16.5 %collective-permute-start = (bf16[1024,256]{1,0:T(8,128)(2,1)}, bf16[1024,256]{1,0:T(8,128)(2,1)S(1)}, u32[]{:S(2)}, u32[]{:S(2)}) collective-permute-start(bf16[1024,256]{1,0:T(8,128)(2,1)} %copy.80), channel_id=1, source_target_pairs={{0,8},{8,16},{16,24},{24,32},{32,40},{40,48},{48,56},{56,64},{64,7... | collective-permute-start | bytes 1572872 | tf_op jit(solution)/shard_map/while/body/eval_jaxpr/ppermute | solution.py:9
  411.2 2.2 copy-start.3
  424.8 10.9 collective-permute-start.1
  424.8 16.5 %collective-permute-start = (bf16[1024,256]{1,0:T(8,128)(2,1)}, bf16[1024,256]{1,0:T(8,128)(2,1)S(1)}, u32[]{:S(2)}, u32[]{:S(2)}) collective-permute-start(bf16[1024,256]{1,0:T(8,128)(2,1)} %copy.80), channel_id=1, source_target_pairs={{0,8},{8,16},{16,24},{24,32},{32,40},{40,48},{48,56},{56,64},{64,7... | collective-permute-start | bytes 1572872 | tf_op jit(solution)/shard_map/while/body/eval_jaxpr/ppermute | solution.py:9
  468.0 10.9 collective-permute-start.1
  468.0 16.5 %collective-permute-start = (bf16[1024,256]{1,0:T(8,128)(2,1)}, bf16[1024,256]{1,0:T(8,128)(2,1)S(1)}, u32[]{:S(2)}, u32[]{:S(2)}) collective-permute-start(bf16[1024,256]{1,0:T(8,128)(2,1)} %copy.80), channel_id=1, source_target_pairs={{0,8},{8,16},{16,24},{24,32},{32,40},{40,48},{48,56},{56,64},{64,7... | collective-permute-start | bytes 1572872 | tf_op jit(solution)/shard_map/while/body/eval_jaxpr/ppermute | solution.py:9
  511.2 10.9 collective-permute-start.1
  511.2 16.5 %collective-permute-start = (bf16[1024,256]{1,0:T(8,128)(2,1)}, bf16[1024,256]{1,0:T(8,128)(2,1)S(1)}, u32[]{:S(2)}, u32[]{:S(2)}) collective-permute-start(bf16[1024,256]{1,0:T(8,128)(2,1)} %copy.80), channel_id=1, source_target_pairs={{0,8},{8,16},{16,24},{24,32},{32,40},{40,48},{48,56},{56,64},{64,7... | collective-permute-start | bytes 1572872 | tf_op jit(solution)/shard_map/while/body/eval_jaxpr/ppermute | solution.py:9
  554.4 10.9 collective-permute-start.1
  554.4 16.5 %collective-permute-start = (bf16[1024,256]{1,0:T(8,128)(2,1)}, bf16[1024,256]{1,0:T(8,128)(2,1)S(1)}, u32[]{:S(2)}, u32[]{:S(2)}) collective-permute-start(bf16[1024,256]{1,0:T(8,128)(2,1)} %copy.80), channel_id=1, source_target_pairs={{0,8},{8,16},{16,24},{24,32},{32,40},{40,48},{48,56},{56,64},{64,7... | collective-permute-start | bytes 1572872 | tf_op jit(solution)/shard_map/while/body/eval_jaxpr/ppermute | solution.py:9
  597.6 10.9 collective-permute-start.1
  597.6 16.5 %collective-permute-start = (bf16[1024,256]{1,0:T(8,128)(2,1)}, bf16[1024,256]{1,0:T(8,128)(2,1)S(1)}, u32[]{:S(2)}, u32[]{:S(2)}) collective-permute-start(bf16[1024,256]{1,0:T(8,128)(2,1)} %copy.80), channel_id=1, source_target_pairs={{0,8},{8,16},{16,24},{24,32},{32,40},{40,48},{48,56},{56,64},{64,7... | collective-permute-start | bytes 1572872 | tf_op jit(solution)/shard_map/while/body/eval_jaxpr/ppermute | solution.py:9
  640.8 10.9 collective-permute-start.1
  640.8 16.5 %collective-permute-start = (bf16[1024,256]{1,0:T(8,128)(2,1)}, bf16[1024,256]{1,0:T(8,128)(2,1)S(1)}, u32[]{:S(2)}, u32[]{:S(2)}) collective-permute-start(bf16[1024,256]{1,0:T(8,128)(2,1)} %copy.80), channel_id=1, source_target_pairs={{0,8},{8,16},{16,24},{24,32},{32,40},{40,48},{48,56},{56,64},{64,7... | collective-permute-start | bytes 1572872 | tf_op jit(solution)/shard_map/while/body/eval_jaxpr/ppermute | solution.py:9
  684.0 10.9 collective-permute-start.1
  684.0 16.5 %collective-permute-start = (bf16[1024,256]{1,0:T(8,128)(2,1)}, bf16[1024,256]{1,0:T(8,128)(2,1)S(1)}, u32[]{:S(2)}, u32[]{:S(2)}) collective-permute-start(bf16[1024,256]{1,0:T(8,128)(2,1)} %copy.80), channel_id=1, source_target_pairs={{0,8},{8,16},{16,24},{24,32},{32,40},{40,48},{48,56},{56,64},{64,7... | collective-permute-start | bytes 1572872 | tf_op jit(solution)/shard_map/while/body/eval_jaxpr/ppermute | solution.py:9
  727.2 10.9 collective-permute-start.1
  727.2 16.5 %collective-permute-start = (bf16[1024,256]{1,0:T(8,128)(2,1)}, bf16[1024,256]{1,0:T(8,128)(2,1)S(1)}, u32[]{:S(2)}, u32[]{:S(2)}) collective-permute-start(bf16[1024,256]{1,0:T(8,128)(2,1)} %copy.80), channel_id=1, source_target_pairs={{0,8},{8,16},{16,24},{24,32},{32,40},{40,48},{48,56},{56,64},{64,7... | collective-permute-start | bytes 1572872 | tf_op jit(solution)/shard_map/while/body/eval_jaxpr/ppermute | solution.py:9
  746.0 735.6 %reduce-scatter.7.cloned.1.call-start = ((), (), s32[]{:S(2)}) async-start(), calls=%async_computation.3 | async-start | bytes 6340608
  (7 other events, 15.3 us)
Sparse Core Ops, SparseCore 0:
  746.2 68.9 reduce-scatter.4
  826.3 655.2 reduce-scatter.6
where the time goes:
time: 1490 us
  waiting for transfers between devices  969 us (65%)
  local copies, waits for them, and re-layouts  243 us (16%)
  matrix products  153 us (10%)
  other arithmetic  68.1 us (5%)
  blocking collectives  35.7 us (2%)
    unnamed x3, waiting for transfers between devices  655 us
    ppermute x32, waiting for transfers between devices, passed_along(): lax.ppermute(value, axis, [(i, (i + by) % devices) for i in range(devices)])  245 us
    gather x16, local copies, waits for them, and re-layouts, key_meta(): key_pos = jnp.take(span_order, span_ids) * half_len + key_ids % half_len  110 us
    gather x16, local copies, waits for them, and re-layouts, key_meta(): return (key_pos, jnp.take(doc_ids, key_pos))  98.5 us
    reduce_scatter x1, waiting for transfers between devices, per_device(): lax.psum_scatter(kv_grads.astype(jnp.bfloat16), 'outer', scatter_dimensio...  69 us
    dot_general x32, matrix products, one_block(): jnp.einsum('ihc,jc->hij', query_heads, key_rows, preferred_element_type=j...  43.8 us
    dot_general x32, matrix products, one_block(): jnp.einsum('ihc,jc->hij', grad_heads, value_rows, preferred_element_type=...  41 us
    dot_general x32, matrix products, one_block(): jnp.einsum('hij,jc->ihc', score_grads, key_rows, preferred_element_type=j...  39 us
  transfers between devices with their start and end apart: 34, of which 34 were waited for; matrix products, arithmetic and copies ran while one was open for 1% of the time, Pallas kernels for 0%

commit v1 on v0

v1 whole, which is shorter than its diff:
```python
import functools

import jax
import jax.numpy as jnp
from jax import lax
from jax.experimental import pallas as pl
from jax.experimental.pallas import tpu as pltpu
from jax.sharding import PartitionSpec as P

CH = 4
SPAN = 64
HD = 128
HEADS = 6
NQ = SPAN * HEADS
MOST_DOC = 2048


def window_kernel(
    tab,
    q_ref,
    og_ref,
    ao_ref,
    lse_ref,
    pos_ref,
    start_ref,
    kv_hbm,
    dq_ref,
    dkv_hbm,
    kbuf,
    acc,
    obuf,
    zbuf,
    qs,
    gs,
    qt,
    gt,
    delta,
    dqt,
    ksem,
    zsem,
    osem,
    *,
    spans,
    wmax,
):
    scale = HD ** (-0.5)
    base = spans
    zrows = zbuf.shape[0]
    zcount = dkv_hbm.shape[0] // zrows
    p = [tab[base + s] for s in range(2)]
    lo = [tab[base + 2 + s] for s in range(2)]
    nch = [(p[s] - lo[s] + CH) // CH for s in range(2)]
    end = [lo[s] + nch[s] * CH for s in range(2)]

    def key_copy(s, i):
        c = tab[jnp.minimum(lo[s] + i, spans - 1)]
        return pltpu.make_async_copy(
            kv_hbm.at[pl.ds(pl.multiple_of(c * SPAN, SPAN), SPAN)],
            kbuf.at[s, pl.ds(pl.multiple_of(i * SPAN, SPAN), SPAN)],
            ksem.at[s, i],
        )

    for s in range(2):

        @pl.loop(0, nch[s] * CH)
        def _(i):
            key_copy(s, i).start()

    zbuf[...] = jnp.zeros_like(zbuf)

    def zero_copy(i):
        return pltpu.make_async_copy(zbuf, dkv_hbm.at[pl.ds(i * zrows, zrows)], zsem.at[i])

    for i in range(zcount):
        zero_copy(i).start()

    for s in range(2):
        rows = slice(s * SPAN, (s + 1) * SPAN)
        for h in range(HEADS):
            cols = slice(h * HD, (h + 1) * HD)
            dst = slice(h * SPAN, (h + 1) * SPAN)
            qs[s, dst, :] = q_ref[rows, cols]
            gs[s, dst, :] = og_ref[rows, cols]
            prod = og_ref[rows, cols].astype(jnp.float32) * ao_ref[rows, cols].astype(jnp.float32)
            dqt[dst, :] = prod
        delta[s] = jnp.sum(dqt[...].T, axis=0, keepdims=True)
        qt[s] = qs[s].T
        gt[s] = gs[s].T

    for s in range(2):
        lse = lse_ref[pl.ds(s, 1), :]
        qpos = pos_ref[pl.ds(s, 1), :]
        qstart = start_ref[pl.ds(s, 1), :]

        def block(j, dq_acc):
            for i in range(CH):
                key_copy(s, j * CH + i).wait()
            first = pl.multiple_of(j * CH * SPAN, CH * SPAN)
            kc = kbuf[s, pl.ds(first, CH * SPAN), :HD]
            vc = kbuf[s, pl.ds(first, CH * SPAN), HD:]
            st = jnp.dot(kc, qt[s], preferred_element_type=jnp.float32)
            dp = jnp.dot(vc, gt[s], preferred_element_type=jnp.float32)
            kpos = (lo[s] + j * CH) * SPAN + lax.broadcasted_iota(jnp.int32, (CH * SPAN, NQ), 0)
            keep = (kpos >= qstart) & (kpos <= qpos)
            prob = jnp.exp(jnp.where(keep, st * scale - lse, -1e30))
            ds = (scale * prob * (dp - delta[s])).astype(jnp.bfloat16)
            pb = prob.astype(jnp.bfloat16)
            dk = jnp.dot(ds, qs[s], preferred_element_type=jnp.float32)
            dv = jnp.dot(pb, gs[s], preferred_element_type=jnp.float32)
            row0 = pl.multiple_of((lo[s] + j * CH) * SPAN, SPAN)
            at = pl.ds(row0, CH * SPAN)
            if s == 0:
                acc[at, :HD] = dk
                acc[at, HD:] = dv
            else:
                krow = row0 + lax.broadcasted_iota(jnp.int32, (CH * SPAN, HD), 0)
                seen = (krow >= lo[0] * SPAN) & (krow < end[0] * SPAN)
                acc[at, :HD] = dk + jnp.where(seen, acc[at, :HD], 0.0)
                acc[at, HD:] = dv + jnp.where(seen, acc[at, HD:], 0.0)
            return dq_acc + lax.dot_general(
                kc, ds, (((0,), (0,)), ((), ())), preferred_element_type=jnp.float32
            )

        total = lax.fori_loop(0, nch[s], block, jnp.zeros((HD, NQ), jnp.float32))
        dqt[...] = total.T
        for h in range(HEADS):
            dq_ref[s * SPAN : (s + 1) * SPAN, h * HD : (h + 1) * HD] = dqt[
                h * SPAN : (h + 1) * SPAN, :
            ].astype(dq_ref.dtype)

    for i in range(zcount):
        zero_copy(i).wait()

    def out_copy(s, i):
        c = tab[jnp.minimum(lo[s] + i, spans - 1)]
        return pltpu.make_async_copy(
            obuf.at[s, pl.ds(pl.multiple_of(i * SPAN, SPAN), SPAN)],
            dkv_hbm.at[pl.ds(pl.multiple_of(c * SPAN, SPAN), SPAN)],
            osem.at[s, i],
        )

    def mine(s, i):
        k = lo[s] + i
        if s == 1:
            return k < spans
        return (k < spans) & ((k < lo[1]) | (k >= end[1]))

    for s in range(2):

        @pl.loop(0, nch[s] * CH)
        def _(i):
            @pl.when(mine(s, i))
            def _():
                row = pl.multiple_of((lo[s] + i) * SPAN, SPAN)
                obuf[s, pl.ds(pl.multiple_of(i * SPAN, SPAN), SPAN), :] = acc[
                    pl.ds(row, SPAN), :
                ].astype(obuf.dtype)
                out_copy(s, i).start()

    for s in range(2):

        @pl.loop(0, nch[s] * CH)
        def _(i):
            @pl.when(mine(s, i))
            def _():
                out_copy(s, i).wait()


def window_grads(tab, q, og, ao, lse2, pos2, start2, kv_all):
    tokens = kv_all.shape[0]
    spans = tokens // SPAN
    wmax = MOST_DOC // SPAN + 1
    wmax = -(-wmax // CH) * CH
    vmem = pl.BlockSpec(memory_space=pltpu.VMEM)
    anyspace = pl.BlockSpec(memory_space=pl.ANY)
    zrows = 1024
    return pl.pallas_call(
        functools.partial(window_kernel, spans=spans, wmax=wmax),
        out_shape=(
            jax.ShapeDtypeStruct(q.shape, jnp.bfloat16),
            jax.ShapeDtypeStruct((tokens, 2 * HD), jnp.bfloat16),
        ),
        in_specs=[pl.BlockSpec(memory_space=pltpu.SMEM)] + [vmem] * 6 + [anyspace],
        out_specs=(vmem, anyspace),
        scratch_shapes=[
            pltpu.VMEM((2, wmax * SPAN, 2 * HD), jnp.bfloat16),
            pltpu.VMEM((tokens + CH * SPAN, 2 * HD), jnp.float32),
            pltpu.VMEM((2, wmax * SPAN, 2 * HD), jnp.bfloat16),
            pltpu.VMEM((zrows, 2 * HD), jnp.bfloat16),
            pltpu.VMEM((2, NQ, HD), jnp.bfloat16),
            pltpu.VMEM((2, NQ, HD), jnp.bfloat16),
            pltpu.VMEM((2, HD, NQ), jnp.bfloat16),
            pltpu.VMEM((2, HD, NQ), jnp.bfloat16),
            pltpu.VMEM((2, 1, NQ), jnp.float32),
            pltpu.VMEM((NQ, HD), jnp.float32),
            pltpu.SemaphoreType.DMA((2, wmax)),
            pltpu.SemaphoreType.DMA((tokens // zrows,)),
            pltpu.SemaphoreType.DMA((2, wmax)),
        ],
        name="window_grads",
    )(tab, q, og, ao, lse2, pos2, start2, kv_all)


def tables(my_index, log_sums, doc_ids, span_order):
    spans = span_order.shape[0]
    ids = jnp.arange(spans, dtype=jnp.int32)
    inverse = jnp.sum(jnp.where(span_order[None, :] == ids[:, None], ids[None, :], 0), axis=1)
    my_spans = lax.dynamic_slice_in_dim(span_order, 2 * my_index, 2)
    docs = jnp.arange(1, 16, dtype=jnp.int32)
    doc_start = jnp.sum((doc_ids[None, :] < docs[:, None]).astype(jnp.int32), axis=1)
    pos = my_spans[:, None] * SPAN + jnp.arange(SPAN, dtype=jnp.int32)[None, :]
    start = jnp.max(
        jnp.where(doc_start[:, None, None] <= pos[None], doc_start[:, None, None], 0), axis=0
    )
    low = start[:, 0] // SPAN
    tab = jnp.concatenate([inverse, my_spans, low]).astype(jnp.int32)
    pos2 = jnp.tile(pos, (1, HEADS))
    start2 = jnp.tile(start, (1, HEADS))
    lse2 = log_sums.reshape(HEADS, 2, SPAN).transpose(1, 0, 2).reshape(2, NQ)
    return tab, lse2, pos2, start2


def per_device(
    layer_input, queries, keys_values, attn_out, out_grad, log_sums, doc_ids, span_order
):
    axes = ("inner", "outer")
    my_index = lax.axis_index(axes)
    kv_all = lax.all_gather(keys_values, axes, axis=0, tiled=True)
    tab, lse2, pos2, start2 = tables(my_index, log_sums, doc_ids, span_order)
    query_grad, kv_part = window_grads(
        tab, queries, out_grad, attn_out, lse2, pos2, start2, kv_all
    )
    kv_total = lax.psum_scatter(kv_part, axes, scatter_dimension=0, tiled=True)
    weight_grad = lax.psum_scatter(
        lax.dot_general(
            layer_input, kv_total, (((0,), (0,)), ((), ())), preferred_element_type=jnp.float32
        ),
        axes,
        scatter_dimension=0,
        tiled=True,
    )
    return (query_grad, kv_total, weight_grad)


def solution(mesh):
    rows = P(("inner", "outer"), None)
    return jax.shard_map(
        per_device,
        mesh=mesh,
        in_specs=(rows, rows, rows, rows, rows, P(None, ("inner", "outer")), P(), P()),
        out_specs=(rows, rows, rows),
        check_vma=False,
    )
```

time: 1490 us -> 1660 us (1.11)
  waiting for transfers between devices: 969 us -> 1620 us
  local copies, waits for them, and re-layouts: 243 us -> 9.4 us
  matrix products: 153 us -> 4.5 us
  other arithmetic: 68.1 us -> 3.55 us
  blocking collectives: 35.7 us -> 0 us
    reduce_scatter x1, waiting for transfers between devices: 69 us -> 663 us  [per_device(): kv_total = lax.psum_scatter(kv_part, axes, scatter_dimension=0, tiled=True)]
    all_gather x0 -> x1, waiting for transfers between devices: none -> 307 us  [per_device(): kv_all = lax.all_gather(keys_values, axes, axis=0, tiled=True)]
    ppermute x32 -> x0, waiting for transfers between devices: 245 us -> none  [passed_along(): lax.ppermute(value, axis, [(i, (i + by) % devices) for i in range(devices)])]
    gather x33 -> x0, local copies, waits for them, and re-layouts: 210 us -> none  [the longest x16 110 us: key_meta(): key_pos = jnp.take(span_order, span_ids) * half_len + key_ids % half_len]
    dot_general x160 -> x0, matrix products: 149 us -> none  [the longest x32 43.8 us: one_block(): jnp.einsum('ihc,jc->hij', query_heads, key_rows, preferred_element_type=j...]
    all_gather x1 -> x0, blocking collectives: 35.7 us -> none  [per_device(): key_group = lax.all_gather(keys_values, 'outer', axis=0, tiled=True)]
    convert_element_type x33 -> x0, other arithmetic: 31.3 us -> none  [the longest x16 17.3 us: hop_inner(): passed_along(grads_now.astype(jnp.bfloat16), 'inner', 1)]
    add x16 -> x2, other arithmetic: 21.2 us -> 0.07 us  [the longest x1 0.07 us: tables(): pos = my_spans[:, None] * SPAN + jnp.arange(SPAN, dtype=jnp.int32)[None, :]]
  transfers between devices with their start and end apart: 34 -> 3, of which waited for: 34 -> 3; matrix products, arithmetic and copies ran while one was open for 1% -> 0% of each run, Pallas kernels for 0% -> 0%
where the time goes in v1:
time: 1660 us
  waiting for transfers between devices  1620 us (98%)
    reduce_scatter x1, waiting for transfers between devices, per_device(): kv_total = lax.psum_scatter(kv_part, axes, scatter_dimension=0, tiled=True)  663 us
    unnamed x4, waiting for transfers between devices  650 us
    all_gather x1, waiting for transfers between devices, per_device(): kv_all = lax.all_gather(keys_values, axes, axis=0, tiled=True)  307 us
  transfers between devices with their start and end apart: 3, of which 3 were waited for; matrix products, arithmetic and copies ran while one was open for 0% of the time, Pallas kernels for 0%

profile of v1, /device:TPU:0, one launch (start us, length us, event | category | flops | bytes accessed | tf_op | source)
XLA Modules:
  0.0 1659.4 jit_solution(16951184541011099968)
XLA Ops:
  7.2 0.0 copy-start
  7.2 0.0 all-gather.2.cloned.1.call-start
  7.2 0.7 all-gather.2.cloned.1.call-update
  7.9 0.0 reduce-scatter.5.cloned.1.call-start
  8.0 0.8 reshape.61
  8.7 0.7 reshape.62.lse_ref
  9.4 0.8 broadcast_multiply_fusion
  10.1 1.2 convert_reduce_fusion
  11.3 0.1 iota_add_fusion
  11.4 0.1 fusion
  11.5 0.7 tile.21.start_ref
  12.2 0.7 tile.9.pos_ref
  12.8 0.1 slice_reduce_fusion
  12.9 0.8 select_reduce_fusion
  13.7 0.7 pad_add_fusion.tab
  14.4 306.5 %all-gather.2.cloned.1.call-done.kv_hbm = bf16[16384,256]{1,0:T(8,128)(2,1)} async-done(((bf16[128,256]{1,0:T(8,128)(2,1)}), bf16[16384,256]{1,0:T(8,128)(2,1)}) %all-gather.2.cloned.1.call-update) | async-done | bytes 8388624 | tf_op jit(solution)/shard_map/all_gather | solution.py:228
  320.9 9.3 window_grads.1
  330.2 0.0 reduce-scatter.5.cloned.1.call-update
  330.3 0.0 reduce-scatter.7.cloned.1.call-start
  330.3 662.6 %reduce-scatter.5.cloned.1.call-done = bf16[128,256]{1,0:T(8,128)(2,1)} async-done(((bf16[16384,256]{1,0:T(8,128)(2,1)}), bf16[128,256]{1,0:T(8,128)(2,1)}) %reduce-scatter.5.cloned.1.call-update) | async-done | bytes 65552 | tf_op jit(solution)/shard_map/reduce_scatter | solution.py:233
  992.9 0.0 copy-done
  992.9 4.5 convolution_bitcast_fusion
  997.4 6.5 copy.24
  1003.9 0.0 reduce-scatter.7.cloned.1.call-update
  1004.0 648.9 %reduce-scatter.7.cloned.1.call-done = f32[48,256]{1,0:T(8,128)} async-done(((f32[6144,256]{1,0:T(8,128)}), f32[48,256]{1,0:T(8,128)}) %reduce-scatter.7.cloned.1.call-update) | async-done | bytes 49168
  (5 shorter events, 0.0 us)
Async XLA Ops:
  7.2 985.7 %copy-start = (bf16[128,6144]{1,0:T(8,128)(2,1)S(1)}, bf16[128,6144]{1,0:T(8,128)(2,1)}, u32[]{:S(2)}) copy-start(bf16[128,6144]{1,0:T(8,128)(2,1)} %param.8) | copy-start | bytes 4718596
  7.2 313.7 %all-gather.2.cloned.1.call-start = ((), (), s32[]{:S(2)}) async-start(), calls=%async_computation.2 | async-start | bytes 8454144 | tf_op jit(solution)/shard_map/all_gather | solution.py:228
  7.9 985.0 %reduce-scatter.5.cloned.1.call-start = ((), (), s32[]{:S(2)}) async-start(), calls=%async_computation.3 | async-start | bytes 8454144 | tf_op jit(solution)/shard_map/reduce_scatter | solution.py:233
  330.3 1322.6 %reduce-scatter.7.cloned.1.call-start = ((), (), s32[]{:S(2)}) async-start(), calls=%async_computation.4 | async-start | bytes 6340608
Sparse Core Ops, SparseCore 0:
  9.7 311.2 all-gather.1
  330.4 662.4 reduce-scatter.4
  1004.1 648.7 reduce-scatter.6

commit v2 on v1

--- a/solution.py
+++ b/solution.py
@@ -204,7 +204,10 @@
 def tables(my_index, log_sums, doc_ids, span_order):
     spans = span_order.shape[0]
     ids = jnp.arange(spans, dtype=jnp.int32)
-    inverse = jnp.sum(jnp.where(span_order[None, :] == ids[:, None], ids[None, :], 0), axis=1)
+    inner, outer = ids // 16, ids // 2 % 8
+    x, z, core, y = outer // 4 * 2 + inner // 8, inner // 2 % 4, inner % 2, outer % 4
+    kept_at = (((core * 4 + x) * 4 + z) * 4 + y) * 2 + ids % 2
+    inverse = jnp.sum(jnp.where(span_order[None, :] == ids[:, None], kept_at[None, :], 0), axis=1)
     my_spans = lax.dynamic_slice_in_dim(span_order, 2 * my_index, 2)
     docs = jnp.arange(1, 16, dtype=jnp.int32)
     doc_start = jnp.sum((doc_ids[None, :] < docs[:, None]).astype(jnp.int32), axis=1)
@@ -220,25 +223,432 @@
     return tab, lse2, pos2, start2
 
 
+ORDERS = (("x", "y", "z"), ("y", "z", "x"), ("z", "x", "y"))
+COLS = 2 * HD
+HALF = {1: pl.ds(0, HD), -1: pl.ds(HD, HD)}
+FULL = pl.ds(0, COLS)
+
+
+def here():
+    i, o = lax.axis_index("inner"), lax.axis_index("outer")
+    return {"x": (o // 4) * 2 + i // 8, "y": o % 4, "z": (i // 2) % 4, "core": i % 2}
+
+
+def device(c):
+    return ((c["x"] % 2) * 8 + c["z"] * 2 + c["core"], (c["x"] // 2) * 4 + c["y"])
+
+
+def moved(c, axis, by):
+    out = dict(c)
+    out[axis] = (c[axis] + by + 4) % 4
+    return out
+
+
+def place(sel, core=None):
+    where = tuple(slice(None) if sel[a] is None else sel[a] for a in "xzy")
+    return where if core is None else (core, *where)
+
+
+def row_parts(rows):
+    first = -(-rows // 3 // 16) * 16
+    sizes = (first, first, rows - 2 * first)
+    return [(sum(sizes[:i]), sizes[i]) for i in range(3)]
+
+
+class Copies:
+    def __init__(self, send_sem, recv_sem):
+        self.send_sem, self.recv_sem, self.all = send_sem, recv_sem, []
+
+    def send(self, src, dst, target):
+        k = len(self.all)
+        copy = pltpu.make_async_remote_copy(
+            src_ref=src,
+            dst_ref=dst,
+            send_sem=self.send_sem.at[k],
+            recv_sem=self.recv_sem.at[k],
+            device_id=device(target),
+            device_id_type=pl.DeviceIdType.MESH,
+        )
+        copy.start()
+        self.all.append(copy)
+        return copy
+
+    def drain(self):
+        for copy in self.all:
+            copy.wait_send()
+
+
+def meet(me):
+    barrier = pltpu.get_barrier_semaphore()
+    partner = dict(me, core=1 - me["core"])
+    others = [moved(me, a, d) for a in "xyz" for d in (1, -1)] + [partner]
+    for other in others:
+        pl.semaphore_signal(
+            barrier, inc=1, device_id=device(other), device_id_type=pl.DeviceIdType.MESH
+        )
+    pl.semaphore_wait(barrier, len(others))
+    return partner
+
+
+GATHER_COPIES = 3 * 40
+
+
+def gather_kernel(kv_ref, out, send_sem, recv_sem, own_sem):
+    me = here()
+    core = me["core"]
+    own = pltpu.make_async_copy(kv_ref, out.at[place(me, core)], own_sem)
+    own.start()
+    partner = meet(me)
+    net = Copies(send_sem, recv_sem)
+    parts = row_parts(kv_ref.shape[0])
+
+    def block(part, sel, cols=FULL):
+        return out.at[(*place(sel, core), pl.ds(*parts[part]), cols)]
+
+    def push(part, sel, axis, by, cols=FULL, src=None):
+        ref = block(part, sel, cols)
+        return net.send(ref if src is None else src, ref, moved(me, axis, by))
+
+    across = []
+
+    def cross(part, sel):
+        ref = block(part, sel)
+        across.append(net.send(ref, ref, partner))
+
+    def both(part, sel, axis):
+        return {d: push(part, sel, axis, d) for d in (1, -1)}
+
+    def relay(part, sel, axis, copies, keep=True):
+        out_copies = {}
+        for d in (1, -1):
+            copies[d].wait_recv()
+            got = dict(sel, **{axis: moved(me, axis, -d)[axis]})
+            out_copies[d] = push(part, got, axis, d, HALF[d])
+            if keep:
+                cross(part, got)
+        return out_copies
+
+    def settle(copies):
+        for d in (1, -1):
+            copies[d].wait_recv()
+
+    colors = range(3)
+    mine = {a: me[a] for a in "xyz"}
+    first = [
+        {
+            d: push(i, mine, ORDERS[i][0], d, src=kv_ref.at[pl.ds(*parts[i]), :])
+            for d in (1, -1)
+        }
+        for i in colors
+    ]
+    second = [relay(i, mine, ORDERS[i][0], first[i], keep=False) for i in colors]
+    own.wait()
+    line = [dict(mine, **{ORDERS[i][0]: None}) for i in colors]
+    plane = []
+    wave = [{} for i in colors]
+
+    def piece(i, by):
+        return dict(line[i], **{ORDERS[i][1]: moved(me, ORDERS[i][1], by)[ORDERS[i][1]]})
+
+    for i in colors:
+        settle(second[i])
+        plane.append(both(i, line[i], ORDERS[i][1]))
+        wave[i][0] = both(i, piece(i, 0), ORDERS[i][2])
+        cross(i, line[i])
+    turn = []
+    for i in colors:
+        turn.append(relay(i, line[i], ORDERS[i][1], plane[i]))
+        for by in (1, -1):
+            wave[i][by] = both(i, piece(i, by), ORDERS[i][2])
+    last = [{} for i in colors]
+    for i in colors:
+        last[i][0] = relay(i, piece(i, 0), ORDERS[i][2], wave[i][0])
+    for i in colors:
+        settle(turn[i])
+        wave[i][2] = both(i, piece(i, 2), ORDERS[i][2])
+        cross(i, piece(i, 2))
+    for by in (1, -1, 2):
+        for i in colors:
+            last[i][by] = relay(i, piece(i, by), ORDERS[i][2], wave[i][by])
+    for by in (0, 1, -1, 2):
+        for i in colors:
+            settle(last[i][by])
+            a3 = ORDERS[i][2]
+            cross(i, dict(piece(i, by), **{a3: moved(me, a3, 2)[a3]}))
+    for copy in across:
+        copy.wait_recv()
+    net.drain()
+
+
+def gather_keys(keys_values):
+    rows = keys_values.shape[0]
+    out = pl.pallas_call(
+        gather_kernel,
+        out_shape=jax.ShapeDtypeStruct((2, 4, 4, 4, rows, COLS), keys_values.dtype),
+        in_specs=[pl.BlockSpec(memory_space=pltpu.VMEM)],
+        out_specs=pl.BlockSpec(memory_space=pl.ANY),
+        scratch_shapes=[
+            pltpu.SemaphoreType.DMA((GATHER_COPIES,)),
+            pltpu.SemaphoreType.DMA((GATHER_COPIES,)),
+            pltpu.SemaphoreType.DMA,
+        ],
+        compiler_params=pltpu.CompilerParams(collective_id=0, has_side_effects=True),
+        name="gather_keys",
+    )(keys_values)
+    return out.reshape(128 * rows, COLS)
+
+
+class Scatter:
+    STEPS = 4 * 2 + 4
+
+    def __init__(self, me, net, mine, other, near, far, near2, far2, near1, far1, rows):
+        self.me, self.net, self.mine, self.other = me, net, mine, other
+        self.buffers = {3: (near, far), 2: (near2, far2), 1: (near1, far1)}
+        self.parts = row_parts(rows)
+        self.spot = {a: me[a] for a in "xyz"}
+        self.flight = {}
+
+    def at(self, i, d1, d2, d3):
+        a1, a2, a3 = ORDERS[i]
+        sel = dict(self.spot)
+        for a, d in ((a1, d1), (a2, d2), (a3, d3)):
+            sel[a] = None if d is None else moved(self.me, a, d)[a]
+        return sel
+
+    def ref(self, buf, i, sel, cols=FULL):
+        return buf.at[(*place(sel), pl.ds(*self.parts[i]), cols)]
+
+    def line(self, i, d2, d3):
+        a1 = ORDERS[i][0]
+        for v in range(4):
+            yield v, dict(self.at(i, 0, d2, d3), **{a1: v})
+
+    def add_core(self, i, d2, d3):
+        for _, sel in self.line(i, d2, d3):
+            ix = (*place(sel), pl.ds(*self.parts[i]), FULL)
+            self.mine[ix] = self.mine[ix] + self.other[ix]
+
+    def slot(self, level, i, key, kind, d):
+        near, far = self.buffers[level]
+        n = self.parts[i][1]
+        side = 0 if d == 1 else 1
+        lead = (i, key, side) if level == 3 else (i, side)
+        if level == 1:
+            tail = (pl.ds(0, n), slice(None))
+        else:
+            tail = (slice(None), pl.ds(0, n), slice(None))
+        return (near if kind == 0 else far).at[(*lead, *tail)], (near if kind == 0 else far), lead
+
+    def level_sel(self, level, i, key, d):
+        if level == 3:
+            return self.at(i, None, key, d)
+        if level == 2:
+            return self.at(i, None, d, 0)
+        return self.at(i, d, 0, 0)
+
+    def blocks(self, level, i, key, d):
+        if level == 3:
+            return list(self.line(i, key, d))
+        if level == 2:
+            return list(self.line(i, d, 0))
+        return [(None, self.at(i, d, 0, 0))]
+
+    def start(self, level, i, key=0):
+        axis = ORDERS[i][level - 1]
+        sel = self.level_sel(level, i, key, 2)
+        for d in (1, -1):
+            dst, _, _ = self.slot(level, i, KEYS.index(key), 0, d)
+            src = self.ref(self.mine, i, sel, HALF[d])
+            self.flight[level, i, key, 0, d] = self.net.send(src, dst, moved(self.me, axis, d))
+
+    def turn(self, level, i, key=0):
+        axis = ORDERS[i][level - 1]
+        n = self.parts[i][1]
+        for d in (1, -1):
+            self.flight[level, i, key, 0, d].wait_recv()
+            _, buf, lead = self.slot(level, i, KEYS.index(key), 0, d)
+            for v, sel in self.blocks(level, i, key, d):
+                ix = (*place(sel), pl.ds(*self.parts[i]), HALF[d])
+                row = (*lead, pl.ds(0, n), slice(None)) if v is None else (*lead, v, pl.ds(0, n), slice(None))
+                self.mine[ix] = self.mine[ix] + buf[row]
+            dst, _, _ = self.slot(level, i, KEYS.index(key), 1, d)
+            src = self.ref(self.mine, i, self.level_sel(level, i, key, d))
+            self.flight[level, i, key, 1, d] = self.net.send(src, dst, moved(self.me, axis, d))
+
+    def close(self, level, i, key=0, write=None):
+        n = self.parts[i][1]
+        for d in (1, -1):
+            self.flight[level, i, key, 1, d].wait_recv()
+        for v, sel in self.blocks(level, i, key, 0):
+            ix = (*place(sel), pl.ds(*self.parts[i]), FULL)
+            total = self.mine[ix].astype(jnp.float32)
+            if level == 3:
+                total = total + self.other[ix].astype(jnp.float32)
+            for d in (1, -1):
+                _, buf, lead = self.slot(level, i, KEYS.index(key), 1, d)
+                row = (*lead, pl.ds(0, n), slice(None)) if v is None else (*lead, v, pl.ds(0, n), slice(None))
+                total = total + buf[row].astype(jnp.float32)
+            if write is not None:
+                write(self.parts[i], total)
+            else:
+                self.mine[ix] = total.astype(self.mine.dtype)
+
+    def run(self, ready, write):
+        colors = range(3)
+        for n, key in enumerate(KEYS):
+            for i in colors:
+                ready(i, key)
+                self.add_core(i, key, 2)
+                self.start(3, i, key)
+                self.add_core(i, key, 1)
+                self.add_core(i, key, -1)
+            if n >= 1:
+                for i in colors:
+                    self.turn(3, i, KEYS[n - 1])
+            if n >= 2:
+                for i in colors:
+                    self.close(3, i, KEYS[n - 2])
+                    if n == 2:
+                        self.start(2, i)
+        for i in colors:
+            self.turn(3, i, KEYS[3])
+        for i in colors:
+            self.close(3, i, KEYS[2])
+            self.turn(2, i)
+        for i in colors:
+            self.close(3, i, KEYS[3])
+        for i in colors:
+            self.close(2, i)
+            self.start(1, i)
+        for i in colors:
+            self.turn(1, i)
+        for i in colors:
+            self.close(1, i, write=write)
+
+
+KEYS = (2, 1, -1, 0)
+SCATTER_COPIES = 3 * (4 * 4 + 4 + 4)
+
+
+def scatter_scratch(rows):
+    top = row_parts(rows)[0][1]
+    return [
+        pltpu.VMEM((4, 4, 4, rows, COLS), jnp.bfloat16),
+        pltpu.VMEM((4, 4, 4, rows, COLS), jnp.bfloat16),
+        pltpu.VMEM((3, 4, 2, 4, top, HD), jnp.bfloat16),
+        pltpu.VMEM((3, 4, 2, 4, top, COLS), jnp.bfloat16),
+        pltpu.VMEM((3, 2, 4, top, HD), jnp.bfloat16),
+        pltpu.VMEM((3, 2, 4, top, COLS), jnp.bfloat16),
+        pltpu.VMEM((3, 2, top, HD), jnp.bfloat16),
+        pltpu.VMEM((3, 2, top, COLS), jnp.bfloat16),
+    ]
+
+
+def scatter_kernel(part_ref, x_ref, kv_out, w_out, *scratch):
+    kv_bufs, w_bufs, w_theirs = scratch[:8], scratch[8:16], scratch[16]
+    send_sem, recv_sem, load_sem = scratch[17:]
+    me = here()
+    core = me["core"]
+    rows, w_rows = kv_out.shape[0], w_out.shape[0]
+    net = Copies(send_sem, recv_sem)
+    job = Scatter(me, net, *kv_bufs, rows)
+    loads, swaps = {}, {}
+    for n, key in enumerate(KEYS):
+        for i in range(3):
+            sel = job.at(i, None, key, None)
+            src = part_ref.at[(*place(sel, core), pl.ds(*job.parts[i]), FULL)]
+            loads[i, key] = pltpu.make_async_copy(
+                src, job.ref(job.mine, i, sel), load_sem.at[3 * n + i]
+            )
+            loads[i, key].start()
+    partner = meet(me)
+    for key in KEYS:
+        for i in range(3):
+            sel = job.at(i, None, key, None)
+            src = part_ref.at[(*place(sel, 1 - core), pl.ds(*job.parts[i]), FULL)]
+            swaps[i, key] = net.send(src, job.ref(job.other, i, sel), partner)
+
+    def ready(i, key):
+        loads[i, key].wait()
+        swaps[i, key].wait_recv()
+
+    def write(part, total):
+        kv_out[pl.ds(*part), :] = total.astype(kv_out.dtype)
+
+    job.run(ready, write)
+
+    kv = kv_out[...]
+    w_job = Scatter(me, net, *w_bufs, w_rows)
+    wide = 8 * w_rows
+
+    def product(buf, which):
+        for xl in range(2):
+            for z in range(4):
+                col = pl.multiple_of((xl * 8 + z * 2 + which) * wide, 128)
+                out = lax.dot_general(
+                    x_ref[:, pl.ds(col, wide)],
+                    kv,
+                    (((0,), (0,)), ((), ())),
+                    preferred_element_type=jnp.float32,
+                ).astype(jnp.bfloat16)
+                for xh in range(2):
+                    for y in range(4):
+                        at = (xh * 4 + y) * w_rows
+                        buf[2 * xh + xl, z, y] = out[at : at + w_rows]
+
+    product(w_theirs, 1 - core)
+    swap = net.send(w_theirs, w_job.other, partner)
+    product(w_job.mine, core)
+    waited = []
+
+    def w_ready(i, key):
+        if not waited:
+            swap.wait_recv()
+            waited.append(1)
+
+    def w_write(part, total):
+        w_out[pl.ds(*part), :] = total
+
+    w_job.run(w_ready, w_write)
+    net.drain()
+
+
+def scatter_grads(kv_part, layer_input):
+    tokens, width = kv_part.shape[0], layer_input.shape[1]
+    rows, w_rows = tokens // 128, width // 128
+    vmem = pl.BlockSpec(memory_space=pltpu.VMEM)
+    copies = 2 * SCATTER_COPIES + 13
+    return pl.pallas_call(
+        scatter_kernel,
+        out_shape=(
+            jax.ShapeDtypeStruct((rows, COLS), jnp.bfloat16),
+            jax.ShapeDtypeStruct((w_rows, COLS), jnp.float32),
+        ),
+        in_specs=[pl.BlockSpec(memory_space=pl.ANY), vmem],
+        out_specs=(vmem, vmem),
+        scratch_shapes=scatter_scratch(rows)
+        + scatter_scratch(w_rows)
+        + [
+            pltpu.VMEM((4, 4, 4, w_rows, COLS), jnp.bfloat16),
+            pltpu.SemaphoreType.DMA((copies,)),
+            pltpu.SemaphoreType.DMA((copies,)),
+            pltpu.SemaphoreType.DMA((12,)),
+        ],
+        compiler_params=pltpu.CompilerParams(collective_id=1, has_side_effects=True),
+        name="scatter_grads",
+    )(kv_part.reshape(2, 4, 4, 4, rows, COLS), layer_input)
+
+
 def per_device(
     layer_input, queries, keys_values, attn_out, out_grad, log_sums, doc_ids, span_order
 ):
-    axes = ("inner", "outer")
-    my_index = lax.axis_index(axes)
-    kv_all = lax.all_gather(keys_values, axes, axis=0, tiled=True)
+    my_index = lax.axis_index(("inner", "outer"))
+    kv_all = gather_keys(keys_values)
     tab, lse2, pos2, start2 = tables(my_index, log_sums, doc_ids, span_order)
     query_grad, kv_part = window_grads(
         tab, queries, out_grad, attn_out, lse2, pos2, start2, kv_all
     )
-    kv_total = lax.psum_scatter(kv_part, axes, scatter_dimension=0, tiled=True)
-    weight_grad = lax.psum_scatter(
-        lax.dot_general(
-            layer_input, kv_total, (((0,), (0,)), ((), ())), preferred_element_type=jnp.float32
-        ),
-        axes,
-        scatter_dimension=0,
-        tiled=True,
-    )
+    kv_total, weight_grad = scatter_grads(kv_part, layer_input)
     return (query_grad, kv_total, weight_grad)
 
 

time: 1660 us -> 124 us (0.07)
  waiting for transfers between devices: 1620 us -> 0 us
  Pallas kernels: 9.31 us -> 112 us
    reduce_scatter x1 -> x0, waiting for transfers between devices: 663 us -> none  [per_device(): kv_total = lax.psum_scatter(kv_part, axes, scatter_dimension=0, tiled=True)]
    unnamed x4 -> x0, waiting for transfers between devices: 650 us -> none
    all_gather x1 -> x0, waiting for transfers between devices: 307 us -> none  [per_device(): kv_all = lax.all_gather(keys_values, axes, axis=0, tiled=True)]
    pallas_call x0 -> x2, Pallas kernels: none -> 102 us  [the longest x1 61.4 us: scatter_grads(): pl.pallas_call(scatter_kernel, out_shape=(jax.ShapeDtypeStruct((rows, COL...]
  transfers between devices with their start and end apart: 3 -> 0, of which waited for: 3 -> 0; matrix products, arithmetic and copies ran while one was open for 0% -> 0% of each run, Pallas kernels for 0% -> 0%
where the time goes in v2:
time: 124 us; the launch traced here: 122 us
  Pallas kernels  112 us (90%)
  local copies, waits for them, and re-layouts  5.76 us (5%)
  other arithmetic  3.58 us (3%)
    pallas_call x1, Pallas kernels, scatter_grads(): pl.pallas_call(scatter_kernel, out_shape=(jax.ShapeDtypeStruct((rows, COL...  61.4 us
    pallas_call x1, Pallas kernels, gather_keys(): pl.pallas_call(gather_kernel, out_shape=jax.ShapeDtypeStruct((2, 4, 4, 4,...  40.3 us
    pallas_call x1, Pallas kernels, window_grads(): pl.pallas_call(functools.partial(window_kernel, spans=spans, wmax=wmax),...  10.6 us
    unnamed x2, local copies, waits for them, and re-layouts  2.89 us

profile of v2, /device:TPU:0, one launch (start us, length us, event | category | flops | bytes accessed | tf_op | source)
XLA Modules:
  0.0 122.3 jit_solution(16030352324065322880)
XLA Ops:
  0.6 1.2 convert_reduce_fusion
  1.8 0.8 broadcast_multiply_fusion
  2.6 0.1 iota_add_fusion
  2.6 0.1 fusion
  2.7 0.1 slice_reduce_fusion
  2.9 0.8 select_reduce_fusion
  3.7 0.7 pad_add_fusion.tab
  4.3 0.8 reshape.189
  5.1 0.7 reshape.190.lse_ref
  5.8 0.7 tile.21.start_ref
  6.4 0.7 tile.9.pos_ref
  7.1 40.3 %gather_keys.1 = bf16[2,4,4,4,128,256]{5,4,3,2,1,0:T(8,128)(2,1)} custom-call(bf16[128,256]{1,0:T(8,128)(2,1)} %kv_ref.1), custom_call_target="tpu_custom_call" | custom-call | tf_op jit(solution)/shard_map/gather_keys/pallas_call | solution.py:385
  47.4 10.6 %window_grads.1 = (bf16[128,768]{1,0:T(8,128)(2,1)}, bf16[16384,256]{1,0:T(8,128)(2,1)}) custom-call(s32[260]{0:T(512)} %pad_add_fusion.tab, bf16[128,768]{1,0:T(8,128)(2,1)} %q_ref.1, bf16[128,768]{1,0:T(8,128)(2,1)} %og_ref.1, bf16[128,768]{1,0:T(8,128)(2,1)} %ao_ref.1, f32[2,384]{1,0:T(2,128)} %reshape.190.lse_ref, s32[2,384]{1,0:T(2,128)} %tile.9.pos_ref, ...), custom_call_target="tpu_custom_call" | custom-call | tf_op jit(solution)/shard_map/window_grads/pallas_call | solution.py:177
  58.0 61.4 %scatter_grads.1 = (bf16[128,256]{1,0:T(8,128)(2,1)}, f32[48,256]{1,0:T(8,128)}) custom-call(bf16[2,4,4,4,128,256]{5,4,3,2,1,0:T(8,128)(2,1)} %bitcast.6, bf16[128,6144]{1,0:T(8,128)(2,1)} %x_ref.1), custom_call_target="tpu_custom_call" | custom-call | tf_op jit(solution)/shard_map/scatter_grads/pallas_call | solution.py:621
  119.4 1.5 %copy.21 = bf16[128,256]{1,0:T(8,128)(2,1)} copy(bf16[128,256]{1,0:T(8,128)(2,1)} %get-tuple-element.17) | data formatting | bytes 131072
  120.9 1.4 %copy.22 = f32[48,256]{1,0:T(8,128)} copy(f32[48,256]{1,0:T(8,128)} %get-tuple-element.18) | data formatting | bytes 98304
  (6 shorter events, 0.0 us)

commit v3 on v2

--- a/solution.py
+++ b/solution.py
@@ -281,7 +281,7 @@
 def meet(me):
     barrier = pltpu.get_barrier_semaphore()
     partner = dict(me, core=1 - me["core"])
-    others = [moved(me, a, d) for a in "xyz" for d in (1, -1)] + [partner]
+    others = [moved(me, a, d) for a in "xyz" for d in (1, -1, 2)] + [partner]
     for other in others:
         pl.semaphore_signal(
             barrier, inc=1, device_id=device(other), device_id_type=pl.DeviceIdType.MESH
@@ -290,10 +290,10 @@
     return partner
 
 
-GATHER_COPIES = 3 * 40
-
-
-def gather_kernel(kv_ref, out, send_sem, recv_sem, own_sem):
+GATHER_COPIES = 3 * (3 + 3 + 16 + 16)
+
+
+def gather_kernel(kv_ref, out, send_sem, recv_sem, own_sem, aside=lambda: None):
     me = here()
     core = me["core"]
     own = pltpu.make_async_copy(kv_ref, out.at[place(me, core)], own_sem)
@@ -318,56 +318,51 @@
     def both(part, sel, axis):
         return {d: push(part, sel, axis, d) for d in (1, -1)}
 
-    def relay(part, sel, axis, copies, keep=True):
+    def relay(part, sel, axis, copies):
         out_copies = {}
         for d in (1, -1):
             copies[d].wait_recv()
             got = dict(sel, **{axis: moved(me, axis, -d)[axis]})
             out_copies[d] = push(part, got, axis, d, HALF[d])
-            if keep:
-                cross(part, got)
+            cross(part, got)
         return out_copies
 
     def settle(copies):
-        for d in (1, -1):
-            copies[d].wait_recv()
+        for copy in copies.values():
+            copy.wait_recv()
 
     colors = range(3)
     mine = {a: me[a] for a in "xyz"}
     first = [
         {
             d: push(i, mine, ORDERS[i][0], d, src=kv_ref.at[pl.ds(*parts[i]), :])
-            for d in (1, -1)
+            for d in (2, 1, -1)
         }
         for i in colors
     ]
-    second = [relay(i, mine, ORDERS[i][0], first[i], keep=False) for i in colors]
+    aside()
     own.wait()
     line = [dict(mine, **{ORDERS[i][0]: None}) for i in colors]
     plane = []
     wave = [{} for i in colors]
+    last = [{} for i in colors]
 
     def piece(i, by):
         return dict(line[i], **{ORDERS[i][1]: moved(me, ORDERS[i][1], by)[ORDERS[i][1]]})
 
     for i in colors:
-        settle(second[i])
-        plane.append(both(i, line[i], ORDERS[i][1]))
+        settle(first[i])
+        plane.append({d: push(i, line[i], ORDERS[i][1], d) for d in (2, 1, -1)})
+    for i in colors:
         wave[i][0] = both(i, piece(i, 0), ORDERS[i][2])
+    for i in colors:
         cross(i, line[i])
-    turn = []
-    for i in colors:
-        turn.append(relay(i, line[i], ORDERS[i][1], plane[i]))
-        for by in (1, -1):
+    for by in (1, -1, 2):
+        for i in colors:
+            plane[i][by if by == 2 else -by].wait_recv()
             wave[i][by] = both(i, piece(i, by), ORDERS[i][2])
-    last = [{} for i in colors]
-    for i in colors:
-        last[i][0] = relay(i, piece(i, 0), ORDERS[i][2], wave[i][0])
-    for i in colors:
-        settle(turn[i])
-        wave[i][2] = both(i, piece(i, 2), ORDERS[i][2])
-        cross(i, piece(i, 2))
-    for by in (1, -1, 2):
+            cross(i, piece(i, by))
+    for by in (0, 1, -1, 2):
         for i in colors:
             last[i][by] = relay(i, piece(i, by), ORDERS[i][2], wave[i][by])
     for by in (0, 1, -1, 2):
@@ -398,218 +393,202 @@
     return out.reshape(128 * rows, COLS)
 
 
+KEYS = (2, 1, -1, 0)
+AWAY = (2, 1, -1)
+
+
 class Scatter:
-    STEPS = 4 * 2 + 4
-
-    def __init__(self, me, net, mine, other, near, far, near2, far2, near1, far1, rows):
-        self.me, self.net, self.mine, self.other = me, net, mine, other
-        self.buffers = {3: (near, far), 2: (near2, far2), 1: (near1, far1)}
+    def __init__(self, me, net, mine, other, halves, third, second, first, rows):
+        self.me, self.net, self.mine, self.other, self.halves = me, net, mine, other, halves
+        self.buffers = {3: third, 2: second, 1: first}
         self.parts = row_parts(rows)
         self.spot = {a: me[a] for a in "xyz"}
         self.flight = {}
 
     def at(self, i, d1, d2, d3):
-        a1, a2, a3 = ORDERS[i]
         sel = dict(self.spot)
-        for a, d in ((a1, d1), (a2, d2), (a3, d3)):
+        for a, d in zip(ORDERS[i], (d1, d2, d3)):
             sel[a] = None if d is None else moved(self.me, a, d)[a]
         return sel
 
-    def ref(self, buf, i, sel, cols=FULL):
-        return buf.at[(*place(sel), pl.ds(*self.parts[i]), cols)]
-
-    def line(self, i, d2, d3):
-        a1 = ORDERS[i][0]
-        for v in range(4):
-            yield v, dict(self.at(i, 0, d2, d3), **{a1: v})
+    def ix(self, i, sel, cols=FULL):
+        return (*place(sel), pl.ds(*self.parts[i]), cols)
+
+    def level_sel(self, level, i, key, d):
+        return {3: self.at(i, None, key, d), 2: self.at(i, None, d, 0), 1: self.at(i, d, 0, 0)}[level]
+
+    def blocks(self, level, i, key, d):
+        sel = self.level_sel(level, i, key, d)
+        if level == 1:
+            return [((), sel)]
+        return [((v,), dict(sel, **{ORDERS[i][0]: v})) for v in range(4)]
+
+    def lead(self, level, i, key, d):
+        side = AWAY.index(d) if self.halves is None or level < 3 else (0 if d == 1 else 1)
+        return (i, KEYS.index(key), side) if level == 3 else (i, side)
+
+    def slot(self, buf, level, i, key, d):
+        lines = () if level == 1 else (slice(None),)
+        return buf.at[(*self.lead(level, i, key, d), *lines, pl.ds(0, self.parts[i][1]), slice(None))]
+
+    def row(self, level, i, key, d, v):
+        return (*self.lead(level, i, key, d), *v, pl.ds(0, self.parts[i][1]), slice(None))
+
+    def send(self, level, i, key, d):
+        src = self.mine.at[self.ix(i, self.level_sel(level, i, key, d))]
+        dst = self.slot(self.buffers[level], level, i, key, d)
+        to = moved(self.me, ORDERS[i][level - 1], d)
+        self.flight[level, i, key, d] = self.net.send(src, dst, to)
 
     def add_core(self, i, d2, d3):
-        for _, sel in self.line(i, d2, d3):
-            ix = (*place(sel), pl.ds(*self.parts[i]), FULL)
+        for _, sel in self.blocks(3, i, d2, d3):
+            ix = self.ix(i, sel)
             self.mine[ix] = self.mine[ix] + self.other[ix]
 
-    def slot(self, level, i, key, kind, d):
-        near, far = self.buffers[level]
-        n = self.parts[i][1]
-        side = 0 if d == 1 else 1
-        lead = (i, key, side) if level == 3 else (i, side)
-        if level == 1:
-            tail = (pl.ds(0, n), slice(None))
-        else:
-            tail = (slice(None), pl.ds(0, n), slice(None))
-        return (near if kind == 0 else far).at[(*lead, *tail)], (near if kind == 0 else far), lead
-
-    def level_sel(self, level, i, key, d):
-        if level == 3:
-            return self.at(i, None, key, d)
-        if level == 2:
-            return self.at(i, None, d, 0)
-        return self.at(i, d, 0, 0)
-
-    def blocks(self, level, i, key, d):
-        if level == 3:
-            return list(self.line(i, key, d))
-        if level == 2:
-            return list(self.line(i, d, 0))
-        return [(None, self.at(i, d, 0, 0))]
-
-    def start(self, level, i, key=0):
-        axis = ORDERS[i][level - 1]
-        sel = self.level_sel(level, i, key, 2)
+    def open(self, i, key):
+        if self.halves is None:
+            for d in AWAY:
+                self.send(3, i, key, d)
+            return
+        self.add_core(i, key, 2)
+        sel = self.level_sel(3, i, key, 2)
         for d in (1, -1):
-            dst, _, _ = self.slot(level, i, KEYS.index(key), 0, d)
-            src = self.ref(self.mine, i, sel, HALF[d])
-            self.flight[level, i, key, 0, d] = self.net.send(src, dst, moved(self.me, axis, d))
-
-    def turn(self, level, i, key=0):
-        axis = ORDERS[i][level - 1]
-        n = self.parts[i][1]
+            dst = self.slot(self.halves, 3, i, key, d)
+            src = self.mine.at[self.ix(i, sel, HALF[d])]
+            to = moved(self.me, ORDERS[i][2], d)
+            self.flight["half", i, key, d] = self.net.send(src, dst, to)
+        self.add_core(i, key, 1)
+        self.add_core(i, key, -1)
+
+    def turn(self, i, key):
         for d in (1, -1):
-            self.flight[level, i, key, 0, d].wait_recv()
-            _, buf, lead = self.slot(level, i, KEYS.index(key), 0, d)
-            for v, sel in self.blocks(level, i, key, d):
-                ix = (*place(sel), pl.ds(*self.parts[i]), HALF[d])
-                row = (*lead, pl.ds(0, n), slice(None)) if v is None else (*lead, v, pl.ds(0, n), slice(None))
-                self.mine[ix] = self.mine[ix] + buf[row]
-            dst, _, _ = self.slot(level, i, KEYS.index(key), 1, d)
-            src = self.ref(self.mine, i, self.level_sel(level, i, key, d))
-            self.flight[level, i, key, 1, d] = self.net.send(src, dst, moved(self.me, axis, d))
+            self.flight["half", i, key, d].wait_recv()
+            for v, sel in self.blocks(3, i, key, d):
+                ix = self.ix(i, sel, HALF[d])
+                self.mine[ix] = self.mine[ix] + self.halves[self.row(3, i, key, d, v)]
+            self.send(3, i, key, d)
 
     def close(self, level, i, key=0, write=None):
-        n = self.parts[i][1]
-        for d in (1, -1):
-            self.flight[level, i, key, 1, d].wait_recv()
+        sides = (1, -1) if level == 3 and self.halves is not None else AWAY
+        for d in sides:
+            self.flight[level, i, key, d].wait_recv()
         for v, sel in self.blocks(level, i, key, 0):
-            ix = (*place(sel), pl.ds(*self.parts[i]), FULL)
+            ix = self.ix(i, sel)
             total = self.mine[ix].astype(jnp.float32)
-            if level == 3:
+            if level == 3 and self.other is not None:
                 total = total + self.other[ix].astype(jnp.float32)
-            for d in (1, -1):
-                _, buf, lead = self.slot(level, i, KEYS.index(key), 1, d)
-                row = (*lead, pl.ds(0, n), slice(None)) if v is None else (*lead, v, pl.ds(0, n), slice(None))
-                total = total + buf[row].astype(jnp.float32)
-            if write is not None:
+            for d in sides:
+                total = total + self.buffers[level][self.row(level, i, key, d, v)].astype(jnp.float32)
+            if write is None:
+                self.mine[ix] = total.astype(self.mine.dtype)
+            else:
                 write(self.parts[i], total)
-            else:
-                self.mine[ix] = total.astype(self.mine.dtype)
-
-    def run(self, ready, write):
+
+    def finish(self, i, key):
+        self.close(3, i, key)
+        if key != 0:
+            self.send(2, i, 0, key)
+
+    def run(self, ready, write, aside):
         colors = range(3)
-        for n, key in enumerate(KEYS):
-            for i in colors:
-                ready(i, key)
-                self.add_core(i, key, 2)
-                self.start(3, i, key)
-                self.add_core(i, key, 1)
-                self.add_core(i, key, -1)
-            if n >= 1:
+        lag = 1 if self.halves is None else 2
+        for n in range(len(KEYS) + lag):
+            if n < len(KEYS):
                 for i in colors:
-                    self.turn(3, i, KEYS[n - 1])
-            if n >= 2:
+                    ready(i, KEYS[n])
+                    self.open(i, KEYS[n])
+            if lag == 2 and 1 <= n <= len(KEYS):
                 for i in colors:
-                    self.close(3, i, KEYS[n - 2])
-                    if n == 2:
-                        self.start(2, i)
-        for i in colors:
-            self.turn(3, i, KEYS[3])
-        for i in colors:
-            self.close(3, i, KEYS[2])
-            self.turn(2, i)
-        for i in colors:
-            self.close(3, i, KEYS[3])
+                    self.turn(i, KEYS[n - 1])
+            if n == len(KEYS) - 1:
+                aside()
+            if n >= lag:
+                for i in colors:
+                    self.finish(i, KEYS[n - lag])
         for i in colors:
             self.close(2, i)
-            self.start(1, i)
-        for i in colors:
-            self.turn(1, i)
+            for d in AWAY:
+                self.send(1, i, 0, d)
         for i in colors:
             self.close(1, i, write=write)
 
 
-KEYS = (2, 1, -1, 0)
-SCATTER_COPIES = 3 * (4 * 4 + 4 + 4)
-
-
-def scatter_scratch(rows):
+def scatter_scratch(rows, relayed):
     top = row_parts(rows)[0][1]
-    return [
-        pltpu.VMEM((4, 4, 4, rows, COLS), jnp.bfloat16),
-        pltpu.VMEM((4, 4, 4, rows, COLS), jnp.bfloat16),
-        pltpu.VMEM((3, 4, 2, 4, top, HD), jnp.bfloat16),
-        pltpu.VMEM((3, 4, 2, 4, top, COLS), jnp.bfloat16),
-        pltpu.VMEM((3, 2, 4, top, HD), jnp.bfloat16),
-        pltpu.VMEM((3, 2, 4, top, COLS), jnp.bfloat16),
-        pltpu.VMEM((3, 2, top, HD), jnp.bfloat16),
-        pltpu.VMEM((3, 2, top, COLS), jnp.bfloat16),
+    plane = pltpu.VMEM((4, 4, 4, rows, COLS), jnp.bfloat16)
+    return ([plane, plane, pltpu.VMEM((3, 4, 2, 4, top, HD), jnp.bfloat16)] if relayed else [plane]) + [
+        pltpu.VMEM((3, 4, 2 if relayed else 3, 4, top, COLS), jnp.bfloat16),
+        pltpu.VMEM((3, 3, 4, top, COLS), jnp.bfloat16),
+        pltpu.VMEM((3, 3, top, COLS), jnp.bfloat16),
     ]
 
 
+SCATTER_COPIES = 3 * (4 * 4 + 3 + 3) + 3 * (4 * 3 + 3 + 3) + 12 + 8 + 1
+
+
 def scatter_kernel(part_ref, x_ref, kv_out, w_out, *scratch):
-    kv_bufs, w_bufs, w_theirs = scratch[:8], scratch[8:16], scratch[16]
-    send_sem, recv_sem, load_sem = scratch[17:]
+    kv_bufs, w_bufs = scratch[:6], scratch[6:10]
+    x_theirs, xt, pair, send_sem, recv_sem, load_sem = scratch[10:]
     me = here()
     core = me["core"]
     rows, w_rows = kv_out.shape[0], w_out.shape[0]
+    wide = 8 * w_rows
     net = Copies(send_sem, recv_sem)
     job = Scatter(me, net, *kv_bufs, rows)
+    w_job = Scatter(me, net, w_bufs[0], None, None, *w_bufs[1:], w_rows)
     loads, swaps = {}, {}
     for n, key in enumerate(KEYS):
         for i in range(3):
             sel = job.at(i, None, key, None)
             src = part_ref.at[(*place(sel, core), pl.ds(*job.parts[i]), FULL)]
-            loads[i, key] = pltpu.make_async_copy(
-                src, job.ref(job.mine, i, sel), load_sem.at[3 * n + i]
-            )
+            dst = job.mine.at[job.ix(i, sel)]
+            loads[i, key] = pltpu.make_async_copy(src, dst, load_sem.at[3 * n + i])
             loads[i, key].start()
     partner = meet(me)
     for key in KEYS:
         for i in range(3):
             sel = job.at(i, None, key, None)
             src = part_ref.at[(*place(sel, 1 - core), pl.ds(*job.parts[i]), FULL)]
-            swaps[i, key] = net.send(src, job.ref(job.other, i, sel), partner)
+            swaps[i, key] = net.send(src, job.other.at[job.ix(i, sel)], partner)
+
+    def columns(j, which):
+        first = (j // 4 * 8 + j % 4 * 2 + which) * wide
+        return x_ref.at[:, pl.ds(pl.multiple_of(first, 128), wide)]
+
+    x_swaps = [net.send(columns(j, 1 - core), x_theirs.at[j], partner) for j in range(8)]
+    for j in range(8):
+        xt[j, :, :rows] = columns(j, core)[...].T
 
     def ready(i, key):
         loads[i, key].wait()
         swaps[i, key].wait_recv()
 
+    def turn_inputs():
+        for j in range(8):
+            x_swaps[j].wait_recv()
+            xt[j, :, rows:] = x_theirs[j].T
+
     def write(part, total):
-        kv_out[pl.ds(*part), :] = total.astype(kv_out.dtype)
-
-    job.run(ready, write)
-
-    kv = kv_out[...]
-    w_job = Scatter(me, net, *w_bufs, w_rows)
-    wide = 8 * w_rows
-
-    def product(buf, which):
-        for xl in range(2):
-            for z in range(4):
-                col = pl.multiple_of((xl * 8 + z * 2 + which) * wide, 128)
-                out = lax.dot_general(
-                    x_ref[:, pl.ds(col, wide)],
-                    kv,
-                    (((0,), (0,)), ((), ())),
-                    preferred_element_type=jnp.float32,
-                ).astype(jnp.bfloat16)
-                for xh in range(2):
-                    for y in range(4):
-                        at = (xh * 4 + y) * w_rows
-                        buf[2 * xh + xl, z, y] = out[at : at + w_rows]
-
-    product(w_theirs, 1 - core)
-    swap = net.send(w_theirs, w_job.other, partner)
-    product(w_job.mine, core)
-    waited = []
-
-    def w_ready(i, key):
-        if not waited:
-            swap.wait_recv()
-            waited.append(1)
+        low = total.astype(kv_out.dtype)
+        kv_out[pl.ds(*part), :] = low
+        pair[pl.ds(*part), :] = low
+
+    job.run(ready, write, turn_inputs)
+
+    swap = net.send(pair.at[pl.ds(0, rows)], pair.at[pl.ds(rows, rows)], partner)
+    swap.wait_recv()
+    both = pair[...]
+    for j in range(8):
+        out = jnp.dot(xt[j], both, preferred_element_type=jnp.float32).astype(jnp.bfloat16)
+        for xh in range(2):
+            for y in range(4):
+                first = (xh * 4 + y) * w_rows
+                w_job.mine[2 * xh + j // 4, j % 4, y] = out[first : first + w_rows]
 
     def w_write(part, total):
         w_out[pl.ds(*part), :] = total
 
-    w_job.run(w_ready, w_write)
+    w_job.run(lambda i, key: None, w_write, lambda: None)
     net.drain()
 
 
@@ -617,7 +596,6 @@
     tokens, width = kv_part.shape[0], layer_input.shape[1]
     rows, w_rows = tokens // 128, width // 128
     vmem = pl.BlockSpec(memory_space=pltpu.VMEM)
-    copies = 2 * SCATTER_COPIES + 13
     return pl.pallas_call(
         scatter_kernel,
         out_shape=(
@@ -626,12 +604,14 @@
         ),
         in_specs=[pl.BlockSpec(memory_space=pl.ANY), vmem],
         out_specs=(vmem, vmem),
-        scratch_shapes=scatter_scratch(rows)
-        + scatter_scratch(w_rows)
+        scratch_shapes=scatter_scratch(rows, True)
+        + scatter_scratch(w_rows, False)
         + [
-            pltpu.VMEM((4, 4, 4, w_rows, COLS), jnp.bfloat16),
-            pltpu.SemaphoreType.DMA((copies,)),
-            pltpu.SemaphoreType.DMA((copies,)),
+            pltpu.VMEM((8, rows, 8 * w_rows), jnp.bfloat16),
+            pltpu.VMEM((8, 8 * w_rows, 2 * rows), jnp.bfloat16),
+            pltpu.VMEM((2 * rows, COLS), jnp.bfloat16),
+            pltpu.SemaphoreType.DMA((SCATTER_COPIES,)),
+            pltpu.SemaphoreType.DMA((SCATTER_COPIES,)),
             pltpu.SemaphoreType.DMA((12,)),
         ],
         compiler_params=pltpu.CompilerParams(collective_id=1, has_side_effects=True),

time: 124 us -> 109 us (0.88); the launches traced: 122 us -> 109 us
  Pallas kernels: 112 us -> 98.5 us
    pallas_call x1, Pallas kernels: 61.4 us -> 54.7 us  [scatter_grads(): pl.pallas_call(scatter_kernel, out_shape=(jax.ShapeDtypeStruct((rows, COL...]
    pallas_call x1, Pallas kernels: 40.3 us -> 34.5 us  [gather_keys(): pl.pallas_call(gather_kernel, out_shape=jax.ShapeDtypeStruct((2, 4, 4, 4,...]
    pallas_call x1, Pallas kernels: 10.6 us -> 9.32 us  [window_grads(): pl.pallas_call(functools.partial(window_kernel, spans=spans, wmax=wmax),...]
where the time goes in v3:
time: 109 us
  Pallas kernels  98.5 us (90%)
  local copies, waits for them, and re-layouts  5.76 us (5%)
  other arithmetic  3.58 us (3%)
    pallas_call x1, Pallas kernels, scatter_grads(): pl.pallas_call(scatter_kernel, out_shape=(jax.ShapeDtypeStruct((rows, COL...  54.7 us
    pallas_call x1, Pallas kernels, gather_keys(): pl.pallas_call(gather_kernel, out_shape=jax.ShapeDtypeStruct((2, 4, 4, 4,...  34.5 us
    pallas_call x1, Pallas kernels, window_grads(): pl.pallas_call(functools.partial(window_kernel, spans=spans, wmax=wmax),...  9.32 us
    unnamed x2, local copies, waits for them, and re-layouts  2.89 us

profile of v3, /device:TPU:0, one launch (start us, length us, event | category | flops | bytes accessed | tf_op | source)
XLA Modules:
  0.0 108.6 jit_solution(15404475416208222717)
XLA Ops:
  0.6 1.2 %convert_reduce_fusion = s32[15]{0:T(128)S(1)} fusion(s32[16384]{0:T(1024)} %param.14, s32[15]{0:T(128)S(1)} %iota_add_fusion.1), kind=kLoop, calls=%fused_computation | loop fusion | flops 737265 | bytes 65656 | tf_op jit(solution)/shard_map/reduce_sum | solution.py:213
  1.8 0.8 broadcast_multiply_fusion
  2.6 0.1 iota_add_fusion
  2.6 0.1 fusion
  2.7 0.1 slice_reduce_fusion
  2.9 0.8 select_reduce_fusion
  3.7 0.7 pad_add_fusion.tab
  4.3 0.8 reshape.189
  5.1 0.7 reshape.190.lse_ref
  5.8 0.7 tile.21.start_ref
  6.4 0.7 tile.9.pos_ref
  7.1 34.5 %gather_keys.1 = bf16[2,4,4,4,128,256]{5,4,3,2,1,0:T(8,128)(2,1)} custom-call(bf16[128,256]{1,0:T(8,128)(2,1)} %kv_ref.1), custom_call_target="tpu_custom_call" | custom-call | tf_op jit(solution)/shard_map/gather_keys/pallas_call | solution.py:380
  41.6 9.3 %window_grads.1 = (bf16[128,768]{1,0:T(8,128)(2,1)}, bf16[16384,256]{1,0:T(8,128)(2,1)}) custom-call(s32[260]{0:T(512)} %pad_add_fusion.tab, bf16[128,768]{1,0:T(8,128)(2,1)} %q_ref.1, bf16[128,768]{1,0:T(8,128)(2,1)} %og_ref.1, bf16[128,768]{1,0:T(8,128)(2,1)} %ao_ref.1, f32[2,384]{1,0:T(2,128)} %reshape.190.lse_ref, s32[2,384]{1,0:T(2,128)} %tile.9.pos_ref, ...), custom_call_target="tpu_custom_call" | custom-call | tf_op jit(solution)/shard_map/window_grads/pallas_call | solution.py:177
  51.0 54.7 %scatter_grads.1 = (bf16[128,256]{1,0:T(8,128)(2,1)}, f32[48,256]{1,0:T(8,128)}) custom-call(bf16[2,4,4,4,128,256]{5,4,3,2,1,0:T(8,128)(2,1)} %bitcast.6, bf16[128,6144]{1,0:T(8,128)(2,1)} %x_ref.1), custom_call_target="tpu_custom_call" | custom-call | tf_op jit(solution)/shard_map/scatter_grads/pallas_call | solution.py:599
  105.7 1.5 %copy.21 = bf16[128,256]{1,0:T(8,128)(2,1)} copy(bf16[128,256]{1,0:T(8,128)(2,1)} %get-tuple-element.17) | data formatting | bytes 131072
  107.1 1.4 %copy.22 = f32[48,256]{1,0:T(8,128)} copy(f32[48,256]{1,0:T(8,128)} %get-tuple-element.18) | data formatting | bytes 98304
  (6 shorter events, 0.0 us)

commit v4 on v3

--- a/solution.py
+++ b/solution.py
@@ -17,12 +17,12 @@
 
 def window_kernel(
     tab,
-    q_ref,
-    og_ref,
-    ao_ref,
-    lse_ref,
-    pos_ref,
-    start_ref,
+    meta,
+    fmeta,
+    qs,
+    gs,
+    qt,
+    gt,
     kv_hbm,
     dq_ref,
     dkv_hbm,
@@ -30,30 +30,23 @@
     acc,
     obuf,
     zbuf,
-    qs,
-    gs,
-    qt,
-    gt,
-    delta,
     dqt,
     ksem,
     zsem,
     osem,
     *,
     spans,
-    wmax,
 ):
     scale = HD ** (-0.5)
-    base = spans
     zrows = zbuf.shape[0]
     zcount = dkv_hbm.shape[0] // zrows
-    p = [tab[base + s] for s in range(2)]
-    lo = [tab[base + 2 + s] for s in range(2)]
+    p = [tab[0, spans + s] for s in range(2)]
+    lo = [tab[0, spans + 2 + s] for s in range(2)]
     nch = [(p[s] - lo[s] + CH) // CH for s in range(2)]
     end = [lo[s] + nch[s] * CH for s in range(2)]
 
     def key_copy(s, i):
-        c = tab[jnp.minimum(lo[s] + i, spans - 1)]
+        c = tab[0, jnp.minimum(lo[s] + i, spans - 1)]
         return pltpu.make_async_copy(
             kv_hbm.at[pl.ds(pl.multiple_of(c * SPAN, SPAN), SPAN)],
             kbuf.at[s, pl.ds(pl.multiple_of(i * SPAN, SPAN), SPAN)],
@@ -74,23 +67,12 @@
     for i in range(zcount):
         zero_copy(i).start()
 
+    lane = lax.broadcasted_iota(jnp.int32, (1, NQ), 1)
     for s in range(2):
-        rows = slice(s * SPAN, (s + 1) * SPAN)
-        for h in range(HEADS):
-            cols = slice(h * HD, (h + 1) * HD)
-            dst = slice(h * SPAN, (h + 1) * SPAN)
-            qs[s, dst, :] = q_ref[rows, cols]
-            gs[s, dst, :] = og_ref[rows, cols]
-            prod = og_ref[rows, cols].astype(jnp.float32) * ao_ref[rows, cols].astype(jnp.float32)
-            dqt[dst, :] = prod
-        delta[s] = jnp.sum(dqt[...].T, axis=0, keepdims=True)
-        qt[s] = qs[s].T
-        gt[s] = gs[s].T
-
-    for s in range(2):
-        lse = lse_ref[pl.ds(s, 1), :]
-        qpos = pos_ref[pl.ds(s, 1), :]
-        qstart = start_ref[pl.ds(s, 1), :]
+        delta = fmeta[pl.ds(s, 1), :]
+        lse = fmeta[pl.ds(2 + s, 1), :]
+        qpos = p[s] * SPAN + (lane & (SPAN - 1))
+        qstart = meta[pl.ds(1 + s, 1), pl.ds(0, NQ)]
 
         def block(j, dq_acc):
             for i in range(CH):
@@ -103,7 +85,7 @@
             kpos = (lo[s] + j * CH) * SPAN + lax.broadcasted_iota(jnp.int32, (CH * SPAN, NQ), 0)
             keep = (kpos >= qstart) & (kpos <= qpos)
             prob = jnp.exp(jnp.where(keep, st * scale - lse, -1e30))
-            ds = (scale * prob * (dp - delta[s])).astype(jnp.bfloat16)
+            ds = (scale * prob * (dp - delta)).astype(jnp.bfloat16)
             pb = prob.astype(jnp.bfloat16)
             dk = jnp.dot(ds, qs[s], preferred_element_type=jnp.float32)
             dv = jnp.dot(pb, gs[s], preferred_element_type=jnp.float32)
@@ -132,7 +114,7 @@
         zero_copy(i).wait()
 
     def out_copy(s, i):
-        c = tab[jnp.minimum(lo[s] + i, spans - 1)]
+        c = tab[0, jnp.minimum(lo[s] + i, spans - 1)]
         return pltpu.make_async_copy(
             obuf.at[s, pl.ds(pl.multiple_of(i * SPAN, SPAN), SPAN)],
             dkv_hbm.at[pl.ds(pl.multiple_of(c * SPAN, SPAN), SPAN)],
@@ -166,7 +148,7 @@
                 out_copy(s, i).wait()
 
 
-def window_grads(tab, q, og, ao, lse2, pos2, start2, kv_all):
+def window_grads(meta, fmeta, qs, gs, qt, gt, kv_all):
     tokens = kv_all.shape[0]
     spans = tokens // SPAN
     wmax = MOST_DOC // SPAN + 1
@@ -175,9 +157,9 @@
     anyspace = pl.BlockSpec(memory_space=pl.ANY)
     zrows = 1024
     return pl.pallas_call(
-        functools.partial(window_kernel, spans=spans, wmax=wmax),
+        functools.partial(window_kernel, spans=spans),
         out_shape=(
-            jax.ShapeDtypeStruct(q.shape, jnp.bfloat16),
+            jax.ShapeDtypeStruct((2 * SPAN, HEADS * HD), jnp.bfloat16),
             jax.ShapeDtypeStruct((tokens, 2 * HD), jnp.bfloat16),
         ),
         in_specs=[pl.BlockSpec(memory_space=pltpu.SMEM)] + [vmem] * 6 + [anyspace],
@@ -187,40 +169,63 @@
             pltpu.VMEM((tokens + CH * SPAN, 2 * HD), jnp.float32),
             pltpu.VMEM((2, wmax * SPAN, 2 * HD), jnp.bfloat16),
             pltpu.VMEM((zrows, 2 * HD), jnp.bfloat16),
-            pltpu.VMEM((2, NQ, HD), jnp.bfloat16),
-            pltpu.VMEM((2, NQ, HD), jnp.bfloat16),
-            pltpu.VMEM((2, HD, NQ), jnp.bfloat16),
-            pltpu.VMEM((2, HD, NQ), jnp.bfloat16),
-            pltpu.VMEM((2, 1, NQ), jnp.float32),
             pltpu.VMEM((NQ, HD), jnp.float32),
             pltpu.SemaphoreType.DMA((2, wmax)),
             pltpu.SemaphoreType.DMA((tokens // zrows,)),
             pltpu.SemaphoreType.DMA((2, wmax)),
         ],
         name="window_grads",
-    )(tab, q, og, ao, lse2, pos2, start2, kv_all)
-
-
-def tables(my_index, log_sums, doc_ids, span_order):
-    spans = span_order.shape[0]
-    ids = jnp.arange(spans, dtype=jnp.int32)
-    inner, outer = ids // 16, ids // 2 % 8
-    x, z, core, y = outer // 4 * 2 + inner // 8, inner // 2 % 4, inner % 2, outer % 4
-    kept_at = (((core * 4 + x) * 4 + z) * 4 + y) * 2 + ids % 2
-    inverse = jnp.sum(jnp.where(span_order[None, :] == ids[:, None], kept_at[None, :], 0), axis=1)
-    my_spans = lax.dynamic_slice_in_dim(span_order, 2 * my_index, 2)
-    docs = jnp.arange(1, 16, dtype=jnp.int32)
-    doc_start = jnp.sum((doc_ids[None, :] < docs[:, None]).astype(jnp.int32), axis=1)
-    pos = my_spans[:, None] * SPAN + jnp.arange(SPAN, dtype=jnp.int32)[None, :]
-    start = jnp.max(
-        jnp.where(doc_start[:, None, None] <= pos[None], doc_start[:, None, None], 0), axis=0
-    )
-    low = start[:, 0] // SPAN
-    tab = jnp.concatenate([inverse, my_spans, low]).astype(jnp.int32)
-    pos2 = jnp.tile(pos, (1, HEADS))
-    start2 = jnp.tile(start, (1, HEADS))
-    lse2 = log_sums.reshape(HEADS, 2, SPAN).transpose(1, 0, 2).reshape(2, NQ)
-    return tab, lse2, pos2, start2
+    )(meta, meta, fmeta, qs, gs, qt, gt, kv_all)
+
+
+def prepare(q_ref, og_ref, ao_ref, lse_ref, doc_ref, order_ref, qs, gs, qt, gt, meta, fmeta, tmp):
+    spans = order_ref.shape[0] * order_ref.shape[1]
+    order = jnp.concatenate([order_ref[0:1, :], order_ref[1:2, :]], axis=1).astype(jnp.float32)
+    stored = jnp.broadcast_to(order, (spans, spans)).T
+    lanes = lax.broadcasted_iota(jnp.int32, (spans, spans), 1).astype(jnp.float32)
+    c = lax.broadcasted_iota(jnp.int32, (spans, spans), 0)
+    kept = (
+        ((c >> 4) & 1) * 128
+        + (((c >> 3) & 1) * 2 + ((c >> 7) & 1)) * 32
+        + ((c >> 5) & 3) * 8
+        + ((c >> 1) & 3) * 2
+        + (c & 1)
+    ).astype(jnp.float32)
+    inverse = jnp.sum(jnp.where(stored == lanes, kept, 0.0), axis=0, keepdims=True)
+    docs = doc_ref[...]
+    counts = [
+        jnp.sum(jnp.where(docs < d, 1.0, 0.0), axis=0, keepdims=True) for d in range(16)
+    ]
+    first = jnp.sum(jnp.concatenate(counts, axis=0), axis=1, keepdims=True)
+    mine = 2 * (lax.axis_index("inner") * 8 + lax.axis_index("outer"))
+    spot = lax.broadcasted_iota(jnp.int32, (1, spans), 1)
+    lane = lax.broadcasted_iota(jnp.int32, (1, NQ), 1)
+    tail = jnp.zeros((1, spans), jnp.float32)
+    for s in range(2):
+        span = jnp.sum(jnp.where(spot == mine + s, order, 0.0), axis=1, keepdims=True)
+        pos = span * SPAN + (lane & (SPAN - 1)).astype(jnp.float32)
+        start = jnp.max(jnp.where(first <= pos, first, 0.0), axis=0, keepdims=True)
+        low = (start[:, :1].astype(jnp.int32) >> 6).astype(jnp.float32)
+        tail = jnp.where(spot == s, span, jnp.where(spot == 2 + s, low, tail))
+        meta[1 + s : 2 + s, 0:NQ] = start.astype(jnp.int32)
+    meta[0:1, 0:spans] = inverse.astype(jnp.int32)
+    meta[0:1, spans:] = tail.astype(jnp.int32)
+    for s in range(2):
+        rows = slice(s * SPAN, (s + 1) * SPAN)
+        for h in range(HEADS):
+            cols = slice(h * HD, (h + 1) * HD)
+            dst = slice(h * SPAN, (h + 1) * SPAN)
+            qs[s, dst, :] = q_ref[rows, cols]
+            gs[s, dst, :] = og_ref[rows, cols]
+            tmp[dst, :] = og_ref[rows, cols].astype(jnp.float32) * ao_ref[rows, cols].astype(
+                jnp.float32
+            )
+        fmeta[s : s + 1, :] = jnp.sum(tmp[...].T, axis=0, keepdims=True)
+        fmeta[2 + s : 3 + s, :] = jnp.concatenate(
+            [lse_ref[h : h + 1, rows] for h in range(HEADS)], axis=1
+        )
+        qt[s] = qs[s].T
+        gt[s] = gs[s].T
 
 
 ORDERS = (("x", "y", "z"), ("y", "z", "x"), ("z", "x", "y"))
@@ -293,7 +298,8 @@
 GATHER_COPIES = 3 * (3 + 3 + 16 + 16)
 
 
-def gather_kernel(kv_ref, out, send_sem, recv_sem, own_sem, aside=lambda: None):
+def gather_kernel(kv_ref, *refs):
+    *small, out, tmp, send_sem, recv_sem, own_sem = refs
     me = here()
     core = me["core"]
     own = pltpu.make_async_copy(kv_ref, out.at[place(me, core)], own_sem)
@@ -340,7 +346,7 @@
         }
         for i in colors
     ]
-    aside()
+    prepare(*small, tmp)
     own.wait()
     line = [dict(mine, **{ORDERS[i][0]: None}) for i in colors]
     plane = []
@@ -375,22 +381,41 @@
     net.drain()
 
 
-def gather_keys(keys_values):
+def gather_keys(keys_values, queries, out_grad, attn_out, log_sums, doc_ids, span_order):
     rows = keys_values.shape[0]
-    out = pl.pallas_call(
+    vmem = pl.BlockSpec(memory_space=pltpu.VMEM)
+    *small, out = pl.pallas_call(
         gather_kernel,
-        out_shape=jax.ShapeDtypeStruct((2, 4, 4, 4, rows, COLS), keys_values.dtype),
-        in_specs=[pl.BlockSpec(memory_space=pltpu.VMEM)],
-        out_specs=pl.BlockSpec(memory_space=pl.ANY),
+        out_shape=(
+            jax.ShapeDtypeStruct((2, NQ, HD), jnp.bfloat16),
+            jax.ShapeDtypeStruct((2, NQ, HD), jnp.bfloat16),
+            jax.ShapeDtypeStruct((2, HD, NQ), jnp.bfloat16),
+            jax.ShapeDtypeStruct((2, HD, NQ), jnp.bfloat16),
+            jax.ShapeDtypeStruct((8, 2 * span_order.shape[0]), jnp.int32),
+            jax.ShapeDtypeStruct((8, NQ), jnp.float32),
+            jax.ShapeDtypeStruct((2, 4, 4, 4, rows, COLS), keys_values.dtype),
+        ),
+        in_specs=[vmem] * 7,
+        out_specs=(*[vmem] * 6, pl.BlockSpec(memory_space=pl.ANY)),
         scratch_shapes=[
+            pltpu.VMEM((NQ, HD), jnp.float32),
             pltpu.SemaphoreType.DMA((GATHER_COPIES,)),
             pltpu.SemaphoreType.DMA((GATHER_COPIES,)),
             pltpu.SemaphoreType.DMA,
         ],
         compiler_params=pltpu.CompilerParams(collective_id=0, has_side_effects=True),
         name="gather_keys",
-    )(keys_values)
-    return out.reshape(128 * rows, COLS)
+    )(
+        keys_values,
+        queries,
+        out_grad,
+        attn_out,
+        log_sums,
+        doc_ids.reshape(-1, 128),
+        span_order.reshape(-1, 128),
+    )
+    qs, gs, qt, gt, meta, fmeta = small
+    return meta, fmeta, qs, gs, qt, gt, out.reshape(128 * rows, COLS)
 
 
 KEYS = (2, 1, -1, 0)
@@ -622,11 +647,8 @@
 def per_device(
     layer_input, queries, keys_values, attn_out, out_grad, log_sums, doc_ids, span_order
 ):
-    my_index = lax.axis_index(("inner", "outer"))
-    kv_all = gather_keys(keys_values)
-    tab, lse2, pos2, start2 = tables(my_index, log_sums, doc_ids, span_order)
     query_grad, kv_part = window_grads(
-        tab, queries, out_grad, attn_out, lse2, pos2, start2, kv_all
+        *gather_keys(keys_values, queries, out_grad, attn_out, log_sums, doc_ids, span_order)
     )
     kv_total, weight_grad = scatter_grads(kv_part, layer_input)
     return (query_grad, kv_total, weight_grad)

time: 109 us -> 105 us (0.963)
  other arithmetic: 3.58 us -> 0 us
  local copies, waits for them, and re-layouts: 5.76 us -> 2.89 us
  Pallas kernels: 98.5 us -> 101 us
    pallas_call x1, Pallas kernels: 54.7 us -> 57.3 us  [scatter_grads(): pl.pallas_call(scatter_kernel, out_shape=(jax.ShapeDtypeStruct((rows, COL...]
    reduce_sum x2 -> x0, other arithmetic: 1.95 us -> none  [the longest x1 1.16 us: tables(): jnp.sum((doc_ids[None, :] < docs[:, None]).astype(jnp.int32), axis=1)]
    reshape x3 -> x0, local copies, waits for them, and re-layouts: 1.42 us -> none  [tables(): lse2 = log_sums.reshape(HEADS, 2, SPAN).transpose(1, 0, 2).reshape(2, NQ)]
    another operation x4 -> x0, local copies, waits for them, and re-layouts: 1.32 us -> none  [the longest x2 0.67 us: tables(): start2 = jnp.tile(start, (1, HEADS))]
where the time goes in v4:
time: 105 us; the launch traced here: 104 us
  Pallas kernels  101 us (96%)
  local copies, waits for them, and re-layouts  2.89 us (3%)
    pallas_call x1, Pallas kernels, scatter_grads(): pl.pallas_call(scatter_kernel, out_shape=(jax.ShapeDtypeStruct((rows, COL...  57.3 us
    pallas_call x1, Pallas kernels, gather_keys(): pl.pallas_call(gather_kernel, out_shape=(jax.ShapeDtypeStruct((2, NQ, HD)...  35.9 us
    pallas_call x1, Pallas kernels, window_grads(): pl.pallas_call(functools.partial(window_kernel, spans=spans), out_shape=(...  7.6 us
    unnamed x2, local copies, waits for them, and re-layouts  2.89 us

profile of v4, /device:TPU:0, one launch (start us, length us, event | category | flops | bytes accessed | tf_op | source)
XLA Modules:
  0.0 104.3 jit_solution(3952091830120968446)
XLA Ops:
  0.6 35.9 %gather_keys.1 = (bf16[2,384,128]{2,1,0:T(8,128)(2,1)}, bf16[2,384,128]{2,1,0:T(8,128)(2,1)}, bf16[2,128,384]{2,1,0:T(8,128)(2,1)}, bf16[2,128,384]{2,1,0:T(8,12...) custom-call(bf16[128,256]{1,0:T(8,128)(2,1)} %kv_ref.1, ...), custom_call_target="tpu_custom_call" | custom-call | tf_op jit(solution)/shard_map/gather_keys/pallas_call | solution.py:387
  36.5 7.6 %window_grads.1 = (bf16[128,768]{1,0:T(8,128)(2,1)}, bf16[16384,256]{1,0:T(8,128)(2,1)}) custom-call(s32[8,512]{1,0:T(8,128)} %get-tuple-element.14.tab.meta, s32[8,512]{1,0:T(8,128)} %get-tuple-element.14.tab.meta, f32[8,384]{1,0:T(8,128)} %get-tuple-element.15.fmeta, bf16[2,384,128]{2,1,0:T(8,128)(2,1)} %get-tuple-element.16.qs, ...), custom_call_target="tpu_custom_call" | custom-call | tf_op jit(solution)/shard_map/window_grads/pallas_call | solution.py:159
  44.1 57.3 %scatter_grads.1 = (bf16[128,256]{1,0:T(8,128)(2,1)}, f32[48,256]{1,0:T(8,128)}) custom-call(bf16[2,4,4,4,128,256]{5,4,3,2,1,0:T(8,128)(2,1)} %bitcast.4, bf16[128,6144]{1,0:T(8,128)(2,1)} %x_ref.1), custom_call_target="tpu_custom_call" | custom-call | tf_op jit(solution)/shard_map/scatter_grads/pallas_call | solution.py:624
  101.4 1.5 %copy.13 = bf16[128,256]{1,0:T(8,128)(2,1)} copy(bf16[128,256]{1,0:T(8,128)(2,1)} %get-tuple-element.29) | data formatting | bytes 131072
  102.9 1.4 %copy.14 = f32[48,256]{1,0:T(8,128)} copy(f32[48,256]{1,0:T(8,128)} %get-tuple-element.30) | data formatting | bytes 98304

commit v5 on v4

--- a/solution.py
+++ b/solution.py
@@ -26,8 +26,12 @@
     kv_hbm,
     dq_ref,
     dkv_hbm,
-    kbuf,
-    acc,
+    keys0,
+    keys1,
+    acc0,
+    acc1,
+    dq0,
+    dq1,
     obuf,
     zbuf,
     dqt,
@@ -38,25 +42,27 @@
     spans,
 ):
     scale = HD ** (-0.5)
+    log2e = 1.4426950408889634
+    two = range(2)
+    kbuf, acc, dqs = (keys0, keys1), (acc0, acc1), (dq0, dq1)
     zrows = zbuf.shape[0]
     zcount = dkv_hbm.shape[0] // zrows
-    p = [tab[0, spans + s] for s in range(2)]
-    lo = [tab[0, spans + 2 + s] for s in range(2)]
-    nch = [(p[s] - lo[s] + CH) // CH for s in range(2)]
-    end = [lo[s] + nch[s] * CH for s in range(2)]
+    p = [tab[0, spans + s] for s in two]
+    lo = [tab[0, spans + 2 + s] for s in two]
+    count = [p[s] - lo[s] + 1 for s in two]
+    blocks = (jnp.maximum(count[0], count[1]) + CH - 1) // CH
 
     def key_copy(s, i):
         c = tab[0, jnp.minimum(lo[s] + i, spans - 1)]
         return pltpu.make_async_copy(
             kv_hbm.at[pl.ds(pl.multiple_of(c * SPAN, SPAN), SPAN)],
-            kbuf.at[s, pl.ds(pl.multiple_of(i * SPAN, SPAN), SPAN)],
+            kbuf[s].at[pl.ds(pl.multiple_of(i * SPAN, SPAN), SPAN)],
             ksem.at[s, i],
         )
 
-    for s in range(2):
-
-        @pl.loop(0, nch[s] * CH)
-        def _(i):
+    @pl.loop(0, blocks * CH)
+    def _(i):
+        for s in two:
             key_copy(s, i).start()
 
     zbuf[...] = jnp.zeros_like(zbuf)
@@ -68,84 +74,92 @@
         zero_copy(i).start()
 
     lane = lax.broadcasted_iota(jnp.int32, (1, NQ), 1)
-    for s in range(2):
-        delta = fmeta[pl.ds(s, 1), :]
-        lse = fmeta[pl.ds(2 + s, 1), :]
-        qpos = p[s] * SPAN + (lane & (SPAN - 1))
-        qstart = meta[pl.ds(1 + s, 1), pl.ds(0, NQ)]
-
-        def block(j, dq_acc):
-            for i in range(CH):
+    delta = [fmeta[pl.ds(s, 1), :] for s in two]
+    lse = [fmeta[pl.ds(2 + s, 1), :] * log2e for s in two]
+    qpos = [p[s] * SPAN + (lane & (SPAN - 1)) for s in two]
+    qstart = [meta[pl.ds(1 + s, 1), pl.ds(0, NQ)] for s in two]
+    for s in two:
+        dqs[s][...] = jnp.zeros_like(dqs[s])
+
+    @pl.loop(0, blocks)
+    def _(j):
+        for i in range(CH):
+            for s in two:
                 key_copy(s, j * CH + i).wait()
-            first = pl.multiple_of(j * CH * SPAN, CH * SPAN)
-            kc = kbuf[s, pl.ds(first, CH * SPAN), :HD]
-            vc = kbuf[s, pl.ds(first, CH * SPAN), HD:]
+        first = pl.multiple_of(j * CH * SPAN, CH * SPAN)
+        at = pl.ds(first, CH * SPAN)
+        row = lax.broadcasted_iota(jnp.int32, (CH * SPAN, NQ), 0)
+        for s in two:
+            kc = kbuf[s][at, :HD]
+            vc = kbuf[s][at, HD:]
             st = jnp.dot(kc, qt[s], preferred_element_type=jnp.float32)
             dp = jnp.dot(vc, gt[s], preferred_element_type=jnp.float32)
-            kpos = (lo[s] + j * CH) * SPAN + lax.broadcasted_iota(jnp.int32, (CH * SPAN, NQ), 0)
-            keep = (kpos >= qstart) & (kpos <= qpos)
-            prob = jnp.exp(jnp.where(keep, st * scale - lse, -1e30))
-            ds = (scale * prob * (dp - delta)).astype(jnp.bfloat16)
+            base = (lo[s] + j * CH) * SPAN
+            keep = (row >= qstart[s] - base) & (row <= qpos[s] - base)
+            prob = jnp.exp2(jnp.where(keep, st * (scale * log2e) - lse[s], -1e30))
+            ds = (scale * prob * (dp - delta[s])).astype(jnp.bfloat16)
             pb = prob.astype(jnp.bfloat16)
-            dk = jnp.dot(ds, qs[s], preferred_element_type=jnp.float32)
-            dv = jnp.dot(pb, gs[s], preferred_element_type=jnp.float32)
-            row0 = pl.multiple_of((lo[s] + j * CH) * SPAN, SPAN)
-            at = pl.ds(row0, CH * SPAN)
-            if s == 0:
-                acc[at, :HD] = dk
-                acc[at, HD:] = dv
-            else:
-                krow = row0 + lax.broadcasted_iota(jnp.int32, (CH * SPAN, HD), 0)
-                seen = (krow >= lo[0] * SPAN) & (krow < end[0] * SPAN)
-                acc[at, :HD] = dk + jnp.where(seen, acc[at, :HD], 0.0)
-                acc[at, HD:] = dv + jnp.where(seen, acc[at, HD:], 0.0)
-            return dq_acc + lax.dot_general(
+            acc[s][at, :HD] = jnp.dot(ds, qs[s], preferred_element_type=jnp.float32)
+            acc[s][at, HD:] = jnp.dot(pb, gs[s], preferred_element_type=jnp.float32)
+            dqs[s][...] += lax.dot_general(
                 kc, ds, (((0,), (0,)), ((), ())), preferred_element_type=jnp.float32
             )
 
-        total = lax.fori_loop(0, nch[s], block, jnp.zeros((HD, NQ), jnp.float32))
-        dqt[...] = total.T
-        for h in range(HEADS):
-            dq_ref[s * SPAN : (s + 1) * SPAN, h * HD : (h + 1) * HD] = dqt[
-                h * SPAN : (h + 1) * SPAN, :
-            ].astype(dq_ref.dtype)
-
     for i in range(zcount):
         zero_copy(i).wait()
 
     def out_copy(s, i):
-        c = tab[0, jnp.minimum(lo[s] + i, spans - 1)]
+        c = tab[0, lo[s] + i]
         return pltpu.make_async_copy(
             obuf.at[s, pl.ds(pl.multiple_of(i * SPAN, SPAN), SPAN)],
             dkv_hbm.at[pl.ds(pl.multiple_of(c * SPAN, SPAN), SPAN)],
             osem.at[s, i],
         )
 
-    def mine(s, i):
-        k = lo[s] + i
-        if s == 1:
-            return k < spans
-        return (k < spans) & ((k < lo[1]) | (k >= end[1]))
-
-    for s in range(2):
-
-        @pl.loop(0, nch[s] * CH)
-        def _(i):
-            @pl.when(mine(s, i))
-            def _():
-                row = pl.multiple_of((lo[s] + i) * SPAN, SPAN)
-                obuf[s, pl.ds(pl.multiple_of(i * SPAN, SPAN), SPAN), :] = acc[
-                    pl.ds(row, SPAN), :
-                ].astype(obuf.dtype)
-                out_copy(s, i).start()
-
-    for s in range(2):
-
-        @pl.loop(0, nch[s] * CH)
-        def _(i):
-            @pl.when(mine(s, i))
-            def _():
-                out_copy(s, i).wait()
+    def shared(s, i):
+        other = lo[s] + i - lo[1 - s]
+        return other, (other >= 0) & (other < count[1 - s])
+
+    def rows_of(i):
+        return pl.ds(pl.multiple_of(i * SPAN, SPAN), SPAN)
+
+    @pl.loop(0, count[0])
+    def _(i):
+        other, both = shared(0, i)
+
+        @pl.when(both)
+        def _():
+            obuf[0, rows_of(i), :] = (acc0[rows_of(i), :] + acc1[rows_of(other), :]).astype(obuf.dtype)
+
+        @pl.when(jnp.logical_not(both))
+        def _():
+            obuf[0, rows_of(i), :] = acc0[rows_of(i), :].astype(obuf.dtype)
+
+        out_copy(0, i).start()
+
+    @pl.loop(0, count[1])
+    def _(i):
+        @pl.when(jnp.logical_not(shared(1, i)[1]))
+        def _():
+            obuf[1, rows_of(i), :] = acc1[rows_of(i), :].astype(obuf.dtype)
+            out_copy(1, i).start()
+
+    for s in two:
+        dqt[...] = dqs[s][...].T
+        for h in range(HEADS):
+            dq_ref[s * SPAN : (s + 1) * SPAN, h * HD : (h + 1) * HD] = dqt[
+                h * SPAN : (h + 1) * SPAN, :
+            ].astype(dq_ref.dtype)
+
+    @pl.loop(0, count[0])
+    def _(i):
+        out_copy(0, i).wait()
+
+    @pl.loop(0, count[1])
+    def _(i):
+        @pl.when(jnp.logical_not(shared(1, i)[1]))
+        def _():
+            out_copy(1, i).wait()
 
 
 def window_grads(meta, fmeta, qs, gs, qt, gt, kv_all):
@@ -165,8 +179,12 @@
         in_specs=[pl.BlockSpec(memory_space=pltpu.SMEM)] + [vmem] * 6 + [anyspace],
         out_specs=(vmem, anyspace),
         scratch_shapes=[
-            pltpu.VMEM((2, wmax * SPAN, 2 * HD), jnp.bfloat16),
-            pltpu.VMEM((tokens + CH * SPAN, 2 * HD), jnp.float32),
+            pltpu.VMEM((wmax * SPAN, 2 * HD), jnp.bfloat16),
+            pltpu.VMEM((wmax * SPAN, 2 * HD), jnp.bfloat16),
+            pltpu.VMEM((wmax * SPAN, 2 * HD), jnp.float32),
+            pltpu.VMEM((wmax * SPAN, 2 * HD), jnp.float32),
+            pltpu.VMEM((HD, NQ), jnp.float32),
+            pltpu.VMEM((HD, NQ), jnp.float32),
             pltpu.VMEM((2, wmax * SPAN, 2 * HD), jnp.bfloat16),
             pltpu.VMEM((zrows, 2 * HD), jnp.bfloat16),
             pltpu.VMEM((NQ, HD), jnp.float32),
@@ -299,7 +317,17 @@
 
 
 def gather_kernel(kv_ref, *refs):
-    *small, out, tmp, send_sem, recv_sem, own_sem = refs
+    sources, targets, out = refs[:6], refs[6:12], refs[12]
+    held, made = refs[13:19], refs[19:25]
+    tmp, send_sem, recv_sem, own_sem, small_sem = refs[25:]
+    taken = [
+        pltpu.make_async_copy(sources[k], held[k], small_sem.at[k]) for k in range(6)
+    ]
+    given = [
+        pltpu.make_async_copy(made[k], targets[k], small_sem.at[6 + k]) for k in range(6)
+    ]
+    for copy in taken:
+        copy.start()
     me = here()
     core = me["core"]
     own = pltpu.make_async_copy(kv_ref, out.at[place(me, core)], own_sem)
@@ -346,7 +374,11 @@
         }
         for i in colors
     ]
-    prepare(*small, tmp)
+    for copy in taken:
+        copy.wait()
+    prepare(*held, *made, tmp)
+    for copy in given:
+        copy.start()
     own.wait()
     line = [dict(mine, **{ORDERS[i][0]: None}) for i in colors]
     plane = []
@@ -378,35 +410,16 @@
             cross(i, dict(piece(i, by), **{a3: moved(me, a3, 2)[a3]}))
     for copy in across:
         copy.wait_recv()
+    for copy in given:
+        copy.wait()
     net.drain()
 
 
 def gather_keys(keys_values, queries, out_grad, attn_out, log_sums, doc_ids, span_order):
     rows = keys_values.shape[0]
     vmem = pl.BlockSpec(memory_space=pltpu.VMEM)
-    *small, out = pl.pallas_call(
-        gather_kernel,
-        out_shape=(
-            jax.ShapeDtypeStruct((2, NQ, HD), jnp.bfloat16),
-            jax.ShapeDtypeStruct((2, NQ, HD), jnp.bfloat16),
-            jax.ShapeDtypeStruct((2, HD, NQ), jnp.bfloat16),
-            jax.ShapeDtypeStruct((2, HD, NQ), jnp.bfloat16),
-            jax.ShapeDtypeStruct((8, 2 * span_order.shape[0]), jnp.int32),
-            jax.ShapeDtypeStruct((8, NQ), jnp.float32),
-            jax.ShapeDtypeStruct((2, 4, 4, 4, rows, COLS), keys_values.dtype),
-        ),
-        in_specs=[vmem] * 7,
-        out_specs=(*[vmem] * 6, pl.BlockSpec(memory_space=pl.ANY)),
-        scratch_shapes=[
-            pltpu.VMEM((NQ, HD), jnp.float32),
-            pltpu.SemaphoreType.DMA((GATHER_COPIES,)),
-            pltpu.SemaphoreType.DMA((GATHER_COPIES,)),
-            pltpu.SemaphoreType.DMA,
-        ],
-        compiler_params=pltpu.CompilerParams(collective_id=0, has_side_effects=True),
-        name="gather_keys",
-    )(
-        keys_values,
+    anyspace = pl.BlockSpec(memory_space=pl.ANY)
+    sources = (
         queries,
         out_grad,
         attn_out,
@@ -414,6 +427,34 @@
         doc_ids.reshape(-1, 128),
         span_order.reshape(-1, 128),
     )
+    made = [
+        ((2, NQ, HD), jnp.bfloat16),
+        ((2, NQ, HD), jnp.bfloat16),
+        ((2, HD, NQ), jnp.bfloat16),
+        ((2, HD, NQ), jnp.bfloat16),
+        ((8, 2 * span_order.shape[0]), jnp.int32),
+        ((8, NQ), jnp.float32),
+    ]
+    *small, out = pl.pallas_call(
+        gather_kernel,
+        out_shape=(
+            *[jax.ShapeDtypeStruct(*m) for m in made],
+            jax.ShapeDtypeStruct((2, 4, 4, 4, rows, COLS), keys_values.dtype),
+        ),
+        in_specs=[vmem] + [anyspace] * 6,
+        out_specs=[anyspace] * 7,
+        scratch_shapes=[pltpu.VMEM(v.shape, v.dtype) for v in sources]
+        + [pltpu.VMEM(*m) for m in made]
+        + [
+            pltpu.VMEM((NQ, HD), jnp.float32),
+            pltpu.SemaphoreType.DMA((GATHER_COPIES,)),
+            pltpu.SemaphoreType.DMA((GATHER_COPIES,)),
+            pltpu.SemaphoreType.DMA,
+            pltpu.SemaphoreType.DMA((12,)),
+        ],
+        compiler_params=pltpu.CompilerParams(collective_id=0, has_side_effects=True),
+        name="gather_keys",
+    )(keys_values, *sources)
     qs, gs, qt, gt, meta, fmeta = small
     return meta, fmeta, qs, gs, qt, gt, out.reshape(128 * rows, COLS)
 
@@ -553,7 +594,8 @@
 
 def scatter_kernel(part_ref, x_ref, kv_out, w_out, *scratch):
     kv_bufs, w_bufs = scratch[:6], scratch[6:10]
-    x_theirs, xt, pair, send_sem, recv_sem, load_sem = scratch[10:]
+    x_buf, x_theirs, xt, pair, send_sem, recv_sem, load_sem = scratch[10:]
+    x_load = pltpu.make_async_copy(x_ref, x_buf, load_sem.at[12])
     me = here()
     core = me["core"]
     rows, w_rows = kv_out.shape[0], w_out.shape[0]
@@ -569,6 +611,7 @@
             dst = job.mine.at[job.ix(i, sel)]
             loads[i, key] = pltpu.make_async_copy(src, dst, load_sem.at[3 * n + i])
             loads[i, key].start()
+    x_load.start()
     partner = meet(me)
     for key in KEYS:
         for i in range(3):
@@ -578,8 +621,9 @@
 
     def columns(j, which):
         first = (j // 4 * 8 + j % 4 * 2 + which) * wide
-        return x_ref.at[:, pl.ds(pl.multiple_of(first, 128), wide)]
-
+        return x_buf.at[:, pl.ds(pl.multiple_of(first, 128), wide)]
+
+    x_load.wait()
     x_swaps = [net.send(columns(j, 1 - core), x_theirs.at[j], partner) for j in range(8)]
     for j in range(8):
         xt[j, :, :rows] = columns(j, core)[...].T
@@ -627,17 +671,18 @@
             jax.ShapeDtypeStruct((rows, COLS), jnp.bfloat16),
             jax.ShapeDtypeStruct((w_rows, COLS), jnp.float32),
         ),
-        in_specs=[pl.BlockSpec(memory_space=pl.ANY), vmem],
+        in_specs=[pl.BlockSpec(memory_space=pl.ANY)] * 2,
         out_specs=(vmem, vmem),
         scratch_shapes=scatter_scratch(rows, True)
         + scatter_scratch(w_rows, False)
         + [
+            pltpu.VMEM((rows, width), jnp.bfloat16),
             pltpu.VMEM((8, rows, 8 * w_rows), jnp.bfloat16),
             pltpu.VMEM((8, 8 * w_rows, 2 * rows), jnp.bfloat16),
             pltpu.VMEM((2 * rows, COLS), jnp.bfloat16),
             pltpu.SemaphoreType.DMA((SCATTER_COPIES,)),
             pltpu.SemaphoreType.DMA((SCATTER_COPIES,)),
-            pltpu.SemaphoreType.DMA((12,)),
+            pltpu.SemaphoreType.DMA((13,)),
         ],
         compiler_params=pltpu.CompilerParams(collective_id=1, has_side_effects=True),
         name="scatter_grads",

time: 105 us -> 104 us (level)
    pallas_call x1, Pallas kernels: 7.6 us -> 10.9 us  [window_grads(): pl.pallas_call(functools.partial(window_kernel, spans=spans), out_shape=(...]
    pallas_call x1, Pallas kernels: 57.3 us -> 54.6 us  [scatter_grads(): pl.pallas_call(scatter_kernel, out_shape=(jax.ShapeDtypeStruct((rows, COL...]
    pallas_call x1, Pallas kernels: 35.9 us -> 34.7 us  [gather_keys(): pl.pallas_call(gather_kernel, out_shape=(*[jax.ShapeDtypeStruct(*m) for m...]
where the time goes in v5:
time: 104 us
  Pallas kernels  100 us (96%)
  local copies, waits for them, and re-layouts  2.89 us (3%)
    pallas_call x1, Pallas kernels, scatter_grads(): pl.pallas_call(scatter_kernel, out_shape=(jax.ShapeDtypeStruct((rows, COL...  54.6 us
    pallas_call x1, Pallas kernels, gather_keys(): pl.pallas_call(gather_kernel, out_shape=(*[jax.ShapeDtypeStruct(*m) for m...  34.7 us
    pallas_call x1, Pallas kernels, window_grads(): pl.pallas_call(functools.partial(window_kernel, spans=spans), out_shape=(...  10.9 us
    unnamed x2, local copies, waits for them, and re-layouts  2.89 us

profile of v5, /device:TPU:0, one launch (start us, length us, event | category | flops | bytes accessed | tf_op | source)
XLA Modules:
  0.0 103.8 jit_solution(7549722981478600332)
XLA Ops:
  0.6 34.7 %gather_keys.1 = (bf16[2,384,128]{2,1,0:T(8,128)(2,1)}, bf16[2,384,128]{2,1,0:T(8,128)(2,1)}, bf16[2,128,384]{2,1,0:T(8,128)(2,1)}, bf16[2,128,384]{2,1,0:T(8,12...) custom-call(bf16[128,256]{1,0:T(8,128)(2,1)} %kv_ref.1, ...), custom_call_target="tpu_custom_call" | custom-call | tf_op jit(solution)/shard_map/gather_keys/pallas_call | solution.py:438
  35.4 10.9 %window_grads.1 = (bf16[128,768]{1,0:T(8,128)(2,1)}, bf16[16384,256]{1,0:T(8,128)(2,1)}) custom-call(s32[8,512]{1,0:T(8,128)} %get-tuple-element.14.tab.meta, s32[8,512]{1,0:T(8,128)} %get-tuple-element.14.tab.meta, f32[8,384]{1,0:T(8,128)} %get-tuple-element.15.fmeta, bf16[2,384,128]{2,1,0:T(8,128)(2,1)} %get-tuple-element.16.qs, ...), custom_call_target="tpu_custom_call" | custom-call | tf_op jit(solution)/shard_map/window_grads/pallas_call | solution.py:173
  46.3 54.6 %scatter_grads.1 = (bf16[128,256]{1,0:T(8,128)(2,1)}, f32[48,256]{1,0:T(8,128)}) custom-call(bf16[2,4,4,4,128,256]{5,4,3,2,1,0:T(8,128)(2,1)} %bitcast.4, bf16[128,6144]{1,0:T(8,128)(2,1)} %x_ref.1), custom_call_target="tpu_custom_call" | custom-call | tf_op jit(solution)/shard_map/scatter_grads/pallas_call | solution.py:668
  100.9 1.5 %copy.13 = bf16[128,256]{1,0:T(8,128)(2,1)} copy(bf16[128,256]{1,0:T(8,128)(2,1)} %get-tuple-element.29) | data formatting | bytes 131072
  102.4 1.4 %copy.14 = f32[48,256]{1,0:T(8,128)} copy(f32[48,256]{1,0:T(8,128)} %get-tuple-element.30) | data formatting | bytes 98304

commit v6 on v5

--- a/solution.py
+++ b/solution.py
@@ -32,6 +32,14 @@
     acc1,
     dq0,
     dq1,
+    sc0,
+    sc1,
+    dp0,
+    dp1,
+    ds0,
+    ds1,
+    pb0,
+    pb1,
     obuf,
     zbuf,
     dqt,
@@ -45,6 +53,7 @@
     log2e = 1.4426950408889634
     two = range(2)
     kbuf, acc, dqs = (keys0, keys1), (acc0, acc1), (dq0, dq1)
+    sc, dp, ds, pb = (sc0, sc1), (dp0, dp1), (ds0, ds1), (pb0, pb1)
     zrows = zbuf.shape[0]
     zcount = dkv_hbm.shape[0] // zrows
     p = [tab[0, spans + s] for s in two]
@@ -81,29 +90,64 @@
     for s in two:
         dqs[s][...] = jnp.zeros_like(dqs[s])
 
-    @pl.loop(0, blocks)
-    def _(j):
+    def arrive(j):
         for i in range(CH):
             for s in two:
                 key_copy(s, j * CH + i).wait()
-        first = pl.multiple_of(j * CH * SPAN, CH * SPAN)
-        at = pl.ds(first, CH * SPAN)
-        row = lax.broadcasted_iota(jnp.int32, (CH * SPAN, NQ), 0)
+
+    def block_rows(j):
+        return pl.ds(pl.multiple_of(j * CH * SPAN, CH * SPAN), CH * SPAN)
+
+    def products_in(j, two=two):
+        at = block_rows(j)
         for s in two:
-            kc = kbuf[s][at, :HD]
-            vc = kbuf[s][at, HD:]
-            st = jnp.dot(kc, qt[s], preferred_element_type=jnp.float32)
-            dp = jnp.dot(vc, gt[s], preferred_element_type=jnp.float32)
-            base = (lo[s] + j * CH) * SPAN
-            keep = (row >= qstart[s] - base) & (row <= qpos[s] - base)
-            prob = jnp.exp2(jnp.where(keep, st * (scale * log2e) - lse[s], -1e30))
-            ds = (scale * prob * (dp - delta[s])).astype(jnp.bfloat16)
-            pb = prob.astype(jnp.bfloat16)
-            acc[s][at, :HD] = jnp.dot(ds, qs[s], preferred_element_type=jnp.float32)
-            acc[s][at, HD:] = jnp.dot(pb, gs[s], preferred_element_type=jnp.float32)
+            sc[s][...] = jnp.dot(kbuf[s][at, :HD], qt[s], preferred_element_type=jnp.float32)
+            dp[s][...] = jnp.dot(kbuf[s][at, HD:], gt[s], preferred_element_type=jnp.float32)
+
+    def weigh(j, two=two):
+        part = 16
+        row = lax.broadcasted_iota(jnp.int32, (part, NQ), 0)
+        for n in range(CH * SPAN // part):
+            some = slice(n * part, (n + 1) * part)
+            for s in two:
+                base = (lo[s] + j * CH) * SPAN + n * part
+                keep = (row >= qstart[s] - base) & (row <= qpos[s] - base)
+                score = sc[s][some, :] * (scale * log2e) - lse[s]
+                prob = jnp.exp2(jnp.where(keep, score, -1e30))
+                grad = scale * prob * (dp[s][some, :] - delta[s])
+                ds[s][some, :] = grad.astype(jnp.bfloat16)
+                pb[s][some, :] = prob.astype(jnp.bfloat16)
+
+    def products_out(j, two=two):
+        at = block_rows(j)
+        for s in two:
+            acc[s][at, :HD] = jnp.dot(ds[s][...], qs[s], preferred_element_type=jnp.float32)
+            acc[s][at, HD:] = jnp.dot(pb[s][...], gs[s], preferred_element_type=jnp.float32)
             dqs[s][...] += lax.dot_general(
-                kc, ds, (((0,), (0,)), ((), ())), preferred_element_type=jnp.float32
+                kbuf[s][at, :HD],
+                ds[s][...],
+                (((0,), (0,)), ((), ())),
+                preferred_element_type=jnp.float32,
             )
+
+    for s in two:
+        ds[s][...] = jnp.zeros_like(ds[s])
+        pb[s][...] = jnp.zeros_like(pb[s])
+    arrive(0)
+    products_in(0)
+
+    @pl.loop(0, blocks)
+    def _(j):
+        @pl.when(j + 1 < blocks)
+        def _():
+            arrive(j + 1)
+
+        for s in two:
+            products_out(jnp.maximum(j - 1, 0), (s,))
+            weigh(j, (s,))
+            products_in(jnp.minimum(j + 1, blocks - 1), (s,))
+
+    products_out(blocks - 1)
 
     for i in range(zcount):
         zero_copy(i).wait()
@@ -185,6 +229,8 @@
             pltpu.VMEM((wmax * SPAN, 2 * HD), jnp.float32),
             pltpu.VMEM((HD, NQ), jnp.float32),
             pltpu.VMEM((HD, NQ), jnp.float32),
+            *[pltpu.VMEM((CH * SPAN, NQ), jnp.float32)] * 4,
+            *[pltpu.VMEM((CH * SPAN, NQ), jnp.bfloat16)] * 4,
             pltpu.VMEM((2, wmax * SPAN, 2 * HD), jnp.bfloat16),
             pltpu.VMEM((zrows, 2 * HD), jnp.bfloat16),
             pltpu.VMEM((NQ, HD), jnp.float32),
@@ -689,14 +735,29 @@
     )(kv_part.reshape(2, 4, 4, 4, rows, COLS), layer_input)
 
 
+def copy_kernel(a, b, a_out, b_out):
+    a_out[...] = a[...]
+    b_out[...] = b[...]
+
+
+def handed_on(a, b):
+    vmem = pl.BlockSpec(memory_space=pltpu.VMEM)
+    return pl.pallas_call(
+        copy_kernel,
+        out_shape=[jax.ShapeDtypeStruct(v.shape, v.dtype) for v in (a, b)],
+        in_specs=[vmem] * 2,
+        out_specs=[vmem] * 2,
+        name="handed_on",
+    )(a, b)
+
+
 def per_device(
     layer_input, queries, keys_values, attn_out, out_grad, log_sums, doc_ids, span_order
 ):
     query_grad, kv_part = window_grads(
         *gather_keys(keys_values, queries, out_grad, attn_out, log_sums, doc_ids, span_order)
     )
-    kv_total, weight_grad = scatter_grads(kv_part, layer_input)
-    return (query_grad, kv_total, weight_grad)
+    return (query_grad, *handed_on(*scatter_grads(kv_part, layer_input)))
 
 
 def solution(mesh):

time: 104 us -> 101 us (0.971)
  local copies, waits for them, and re-layouts: 2.89 us -> 0 us
    pallas_call x1, Pallas kernels: 54.6 us -> 51 us  [scatter_grads(): pl.pallas_call(scatter_kernel, out_shape=(jax.ShapeDtypeStruct((rows, COL...]
    unnamed x2 -> x0, local copies, waits for them, and re-layouts: 2.89 us -> none
    pallas_call x0 -> x1, Pallas kernels: none -> 1.49 us  [handed_on(): pl.pallas_call(copy_kernel, out_shape=[jax.ShapeDtypeStruct(v.shape, v.dt...]
    pallas_call x1, Pallas kernels: 10.9 us -> 12 us  [window_grads(): pl.pallas_call(functools.partial(window_kernel, spans=spans), out_shape=(...]
where the time goes in v6:
time: 101 us; the launch traced here: 99.9 us
  Pallas kernels  99.2 us (98%)
    pallas_call x1, Pallas kernels, scatter_grads(): pl.pallas_call(scatter_kernel, out_shape=(jax.ShapeDtypeStruct((rows, COL...  51 us
    pallas_call x1, Pallas kernels, gather_keys(): pl.pallas_call(gather_kernel, out_shape=(*[jax.ShapeDtypeStruct(*m) for m...  34.7 us
    pallas_call x1, Pallas kernels, window_grads(): pl.pallas_call(functools.partial(window_kernel, spans=spans), out_shape=(...  12 us

profile of v6, /device:TPU:0, one launch (start us, length us, event | category | flops | bytes accessed | tf_op | source)
XLA Modules:
  0.0 99.9 jit_solution(4646804045250844854)
XLA Ops:
  0.6 34.7 %gather_keys.1 = (bf16[2,384,128]{2,1,0:T(8,128)(2,1)}, bf16[2,384,128]{2,1,0:T(8,128)(2,1)}, bf16[2,128,384]{2,1,0:T(8,128)(2,1)}, bf16[2,128,384]{2,1,0:T(8,12...) custom-call(bf16[128,256]{1,0:T(8,128)(2,1)} %kv_ref.1, ...), custom_call_target="tpu_custom_call" | custom-call | tf_op jit(solution)/shard_map/gather_keys/pallas_call | solution.py:484
  35.4 12.0 %window_grads.1 = (bf16[128,768]{1,0:T(8,128)(2,1)}, bf16[16384,256]{1,0:T(8,128)(2,1)}) custom-call(s32[8,512]{1,0:T(8,128)} %get-tuple-element.16.tab.meta, s32[8,512]{1,0:T(8,128)} %get-tuple-element.16.tab.meta, f32[8,384]{1,0:T(8,128)} %get-tuple-element.17.fmeta, bf16[2,384,128]{2,1,0:T(8,128)(2,1)} %get-tuple-element.18.qs, ...), custom_call_target="tpu_custom_call" | custom-call | tf_op jit(solution)/shard_map/window_grads/pallas_call | solution.py:217
  47.4 51.0 %scatter_grads.1 = (bf16[128,256]{1,0:T(8,128)(2,1)}, f32[48,256]{1,0:T(8,128)}) custom-call(bf16[2,4,4,4,128,256]{5,4,3,2,1,0:T(8,128)(2,1)} %bitcast.4, bf16[128,6144]{1,0:T(8,128)(2,1)} %x_ref.1), custom_call_target="tpu_custom_call" | custom-call | tf_op jit(solution)/shard_map/scatter_grads/pallas_call | solution.py:714
  98.4 1.5 %handed_on.1 = (bf16[128,256]{1,0:T(8,128)(2,1)}, f32[48,256]{1,0:T(8,128)}) custom-call(bf16[128,256]{1,0:T(8,128)(2,1)} %get-tuple-element.25.a, f32[48,256]{1,0:T(8,128)} %get-tuple-element.26.b), custom_call_target="tpu_custom_call" | custom-call | tf_op jit(solution)/shard_map/handed_on/pallas_call | solution.py:745

commit v7 on v6

--- a/solution.py
+++ b/solution.py
@@ -17,15 +17,22 @@
 
 def window_kernel(
     tab,
+    meta_hbm,
+    fmeta_hbm,
+    qs_hbm,
+    gs_hbm,
+    qt_hbm,
+    gt_hbm,
+    kv_hbm,
+    dq_hbm,
+    dkv_hbm,
     meta,
     fmeta,
     qs,
     gs,
     qt,
     gt,
-    kv_hbm,
     dq_ref,
-    dkv_hbm,
     keys0,
     keys1,
     acc0,
@@ -40,12 +47,12 @@
     ds1,
     pb0,
     pb1,
-    obuf,
     zbuf,
     dqt,
     ksem,
     zsem,
     osem,
+    isem,
     *,
     spans,
 ):
@@ -74,6 +81,13 @@
         for s in two:
             key_copy(s, i).start()
 
+    sources = (meta_hbm, fmeta_hbm, qs_hbm, gs_hbm, qt_hbm, gt_hbm)
+    taken = [
+        pltpu.make_async_copy(src, dst, isem.at[k])
+        for k, (src, dst) in enumerate(zip(sources, (meta, fmeta, qs, gs, qt, gt)))
+    ]
+    for copy in taken:
+        copy.start()
     zbuf[...] = jnp.zeros_like(zbuf)
 
     def zero_copy(i):
@@ -82,6 +96,8 @@
     for i in range(zcount):
         zero_copy(i).start()
 
+    for copy in taken:
+        copy.wait()
     lane = lax.broadcasted_iota(jnp.int32, (1, NQ), 1)
     delta = [fmeta[pl.ds(s, 1), :] for s in two]
     lse = [fmeta[pl.ds(2 + s, 1), :] * log2e for s in two]
@@ -121,8 +137,10 @@
     def products_out(j, two=two):
         at = block_rows(j)
         for s in two:
-            acc[s][at, :HD] = jnp.dot(ds[s][...], qs[s], preferred_element_type=jnp.float32)
-            acc[s][at, HD:] = jnp.dot(pb[s][...], gs[s], preferred_element_type=jnp.float32)
+            dk = jnp.dot(ds[s][...], qs[s], preferred_element_type=jnp.float32)
+            dv = jnp.dot(pb[s][...], gs[s], preferred_element_type=jnp.float32)
+            acc[s][at, :HD] = dk.astype(jnp.bfloat16)
+            acc[s][at, HD:] = dv.astype(jnp.bfloat16)
             dqs[s][...] += lax.dot_general(
                 kbuf[s][at, :HD],
                 ds[s][...],
@@ -149,23 +167,23 @@
 
     products_out(blocks - 1)
 
-    for i in range(zcount):
-        zero_copy(i).wait()
-
     def out_copy(s, i):
         c = tab[0, lo[s] + i]
         return pltpu.make_async_copy(
-            obuf.at[s, pl.ds(pl.multiple_of(i * SPAN, SPAN), SPAN)],
+            acc[s].at[rows_of(i)],
             dkv_hbm.at[pl.ds(pl.multiple_of(c * SPAN, SPAN), SPAN)],
             osem.at[s, i],
         )
 
+    def rows_of(i):
+        return pl.ds(pl.multiple_of(i * SPAN, SPAN), SPAN)
+
     def shared(s, i):
         other = lo[s] + i - lo[1 - s]
         return other, (other >= 0) & (other < count[1 - s])
 
-    def rows_of(i):
-        return pl.ds(pl.multiple_of(i * SPAN, SPAN), SPAN)
+    for i in range(zcount):
+        zero_copy(i).wait()
 
     @pl.loop(0, count[0])
     def _(i):
@@ -173,11 +191,8 @@
 
         @pl.when(both)
         def _():
-            obuf[0, rows_of(i), :] = (acc0[rows_of(i), :] + acc1[rows_of(other), :]).astype(obuf.dtype)
-
-        @pl.when(jnp.logical_not(both))
-        def _():
-            obuf[0, rows_of(i), :] = acc0[rows_of(i), :].astype(obuf.dtype)
+            term = acc0[rows_of(i), :].astype(jnp.float32) + acc1[rows_of(other), :].astype(jnp.float32)
+            acc0[rows_of(i), :] = term.astype(jnp.bfloat16)
 
         out_copy(0, i).start()
 
@@ -185,7 +200,6 @@
     def _(i):
         @pl.when(jnp.logical_not(shared(1, i)[1]))
         def _():
-            obuf[1, rows_of(i), :] = acc1[rows_of(i), :].astype(obuf.dtype)
             out_copy(1, i).start()
 
     for s in two:
@@ -194,6 +208,8 @@
             dq_ref[s * SPAN : (s + 1) * SPAN, h * HD : (h + 1) * HD] = dqt[
                 h * SPAN : (h + 1) * SPAN, :
             ].astype(dq_ref.dtype)
+    dq_out = pltpu.make_async_copy(dq_ref, dq_hbm, isem.at[6])
+    dq_out.start()
 
     @pl.loop(0, count[0])
     def _(i):
@@ -205,13 +221,14 @@
         def _():
             out_copy(1, i).wait()
 
+    dq_out.wait()
+
 
 def window_grads(meta, fmeta, qs, gs, qt, gt, kv_all):
     tokens = kv_all.shape[0]
     spans = tokens // SPAN
     wmax = MOST_DOC // SPAN + 1
     wmax = -(-wmax // CH) * CH
-    vmem = pl.BlockSpec(memory_space=pltpu.VMEM)
     anyspace = pl.BlockSpec(memory_space=pl.ANY)
     zrows = 1024
     return pl.pallas_call(
@@ -220,23 +237,22 @@
             jax.ShapeDtypeStruct((2 * SPAN, HEADS * HD), jnp.bfloat16),
             jax.ShapeDtypeStruct((tokens, 2 * HD), jnp.bfloat16),
         ),
-        in_specs=[pl.BlockSpec(memory_space=pltpu.SMEM)] + [vmem] * 6 + [anyspace],
-        out_specs=(vmem, anyspace),
-        scratch_shapes=[
-            pltpu.VMEM((wmax * SPAN, 2 * HD), jnp.bfloat16),
-            pltpu.VMEM((wmax * SPAN, 2 * HD), jnp.bfloat16),
-            pltpu.VMEM((wmax * SPAN, 2 * HD), jnp.float32),
-            pltpu.VMEM((wmax * SPAN, 2 * HD), jnp.float32),
+        in_specs=[pl.BlockSpec(memory_space=pltpu.SMEM)] + [anyspace] * 7,
+        out_specs=(anyspace, anyspace),
+        scratch_shapes=[pltpu.VMEM(v.shape, v.dtype) for v in (meta, fmeta, qs, gs, qt, gt)]
+        + [
+            pltpu.VMEM((2 * SPAN, HEADS * HD), jnp.bfloat16),
+            *[pltpu.VMEM((wmax * SPAN, 2 * HD), jnp.bfloat16)] * 4,
             pltpu.VMEM((HD, NQ), jnp.float32),
             pltpu.VMEM((HD, NQ), jnp.float32),
             *[pltpu.VMEM((CH * SPAN, NQ), jnp.float32)] * 4,
             *[pltpu.VMEM((CH * SPAN, NQ), jnp.bfloat16)] * 4,
-            pltpu.VMEM((2, wmax * SPAN, 2 * HD), jnp.bfloat16),
             pltpu.VMEM((zrows, 2 * HD), jnp.bfloat16),
             pltpu.VMEM((NQ, HD), jnp.float32),
             pltpu.SemaphoreType.DMA((2, wmax)),
             pltpu.SemaphoreType.DMA((tokens // zrows,)),
             pltpu.SemaphoreType.DMA((2, wmax)),
+            pltpu.SemaphoreType.DMA((7,)),
         ],
         name="window_grads",
     )(meta, meta, fmeta, qs, gs, qt, gt, kv_all)
@@ -553,6 +569,7 @@
         self.flight[level, i, key, d] = self.net.send(src, dst, to)
 
     def add_core(self, i, d2, d3):
+        self.arrived(i, d2, d3)
         for _, sel in self.blocks(3, i, d2, d3):
             ix = self.ix(i, sel)
             self.mine[ix] = self.mine[ix] + self.other[ix]
@@ -582,6 +599,8 @@
 
     def close(self, level, i, key=0, write=None):
         sides = (1, -1) if level == 3 and self.halves is not None else AWAY
+        if level == 3 and self.other is not None:
+            self.arrived(i, key, 0)
         for d in sides:
             self.flight[level, i, key, d].wait_recv()
         for v, sel in self.blocks(level, i, key, 0):
@@ -635,7 +654,7 @@
     ]
 
 
-SCATTER_COPIES = 3 * (4 * 4 + 3 + 3) + 3 * (4 * 3 + 3 + 3) + 12 + 8 + 1
+SCATTER_COPIES = 3 * (4 * 4 + 3 + 3) + 3 * (4 * 3 + 3 + 3) + 21 + 8 + 1
 
 
 def scatter_kernel(part_ref, x_ref, kv_out, w_out, *scratch):
@@ -660,10 +679,18 @@
     x_load.start()
     partner = meet(me)
     for key in KEYS:
-        for i in range(3):
-            sel = job.at(i, None, key, None)
-            src = part_ref.at[(*place(sel, 1 - core), pl.ds(*job.parts[i]), FULL)]
-            swaps[i, key] = net.send(src, job.other.at[job.ix(i, sel)], partner)
+        for d in KEYS if key == KEYS[0] else (None,):
+            for i in range(3):
+                sel = job.at(i, None, key, d)
+                src = part_ref.at[(*place(sel, 1 - core), pl.ds(*job.parts[i]), FULL)]
+                swaps[i, key, d] = net.send(src, job.other.at[job.ix(i, sel)], partner)
+
+    def arrived(i, key, d):
+        copy = swaps.pop((i, key, d if key == KEYS[0] else None), None)
+        if copy is not None:
+            copy.wait_recv()
+
+    job.arrived = arrived
 
     def columns(j, which):
         first = (j // 4 * 8 + j % 4 * 2 + which) * wide
@@ -676,7 +703,6 @@
 
     def ready(i, key):
         loads[i, key].wait()
-        swaps[i, key].wait_recv()
 
     def turn_inputs():
         for j in range(8):

time: 101 us -> 101 us (level)
  no operation moved by 1% of the time
where the time goes in v7:
time: 101 us; the launch traced here: 100 us
  Pallas kernels  99.7 us (99%)
    pallas_call x1, Pallas kernels, scatter_grads(): pl.pallas_call(scatter_kernel, out_shape=(jax.ShapeDtypeStruct((rows, COL...  50.8 us
    pallas_call x1, Pallas kernels, gather_keys(): pl.pallas_call(gather_kernel, out_shape=(*[jax.ShapeDtypeStruct(*m) for m...  34.7 us
    pallas_call x1, Pallas kernels, window_grads(): pl.pallas_call(functools.partial(window_kernel, spans=spans), out_shape=(...  12.7 us

profile of v7, /device:TPU:0, one launch (start us, length us, event | category | flops | bytes accessed | tf_op | source)
XLA Modules:
  0.0 100.3 jit_solution(16817564159974261284)
XLA Ops:
  0.6 34.7 %gather_keys.1 = (bf16[2,384,128]{2,1,0:T(8,128)(2,1)}, bf16[2,384,128]{2,1,0:T(8,128)(2,1)}, bf16[2,128,384]{2,1,0:T(8,128)(2,1)}, bf16[2,128,384]{2,1,0:T(8,12...) custom-call(bf16[128,256]{1,0:T(8,128)(2,1)} %kv_ref.1, ...), custom_call_target="tpu_custom_call" | custom-call | tf_op jit(solution)/shard_map/gather_keys/pallas_call | solution.py:500
  35.4 12.7 %window_grads.1 = (bf16[128,768]{1,0:T(8,128)(2,1)}, bf16[16384,256]{1,0:T(8,128)(2,1)}) custom-call(s32[8,512]{1,0:T(8,128)} %get-tuple-element.16.tab.meta_hbm, s32[8,512]{1,0:T(8,128)} %get-tuple-element.16.tab.meta_hbm, f32[8,384]{1,0:T(8,128)} %get-tuple-element.17.fmeta_hbm, bf16[2,384,128]{2,1,0:T(8,128)(2,1)} %get-tuple-element.18.qs_hbm, ...), custom_call_target="tpu_custom_call" | custom-call | tf_op jit(solution)/shard_map/window_grads/pallas_call | solution.py:234
  48.1 50.8 %scatter_grads.1 = (bf16[128,256]{1,0:T(8,128)(2,1)}, f32[48,256]{1,0:T(8,128)}) custom-call(bf16[2,4,4,4,128,256]{5,4,3,2,1,0:T(8,128)(2,1)} %bitcast.4, bf16[128,6144]{1,0:T(8,128)(2,1)} %x_ref.1), custom_call_target="tpu_custom_call" | custom-call | tf_op jit(solution)/shard_map/scatter_grads/pallas_call | solution.py:740
  98.9 1.5 %handed_on.1 = (bf16[128,256]{1,0:T(8,128)(2,1)}, f32[48,256]{1,0:T(8,128)}) custom-call(bf16[128,256]{1,0:T(8,128)(2,1)} %get-tuple-element.25.a, f32[48,256]{1,0:T(8,128)} %get-tuple-element.26.b), custom_call_target="tpu_custom_call" | custom-call | tf_op jit(solution)/shard_map/handed_on/pallas_call | solution.py:771

commit v8 on v7

--- a/solution.py
+++ b/solution.py
@@ -24,6 +24,7 @@
     qt_hbm,
     gt_hbm,
     kv_hbm,
+    blank,
     dq_hbm,
     dkv_hbm,
     meta,
@@ -47,10 +48,8 @@
     ds1,
     pb0,
     pb1,
-    zbuf,
     dqt,
     ksem,
-    zsem,
     osem,
     isem,
     *,
@@ -61,8 +60,6 @@
     two = range(2)
     kbuf, acc, dqs = (keys0, keys1), (acc0, acc1), (dq0, dq1)
     sc, dp, ds, pb = (sc0, sc1), (dp0, dp1), (ds0, ds1), (pb0, pb1)
-    zrows = zbuf.shape[0]
-    zcount = dkv_hbm.shape[0] // zrows
     p = [tab[0, spans + s] for s in two]
     lo = [tab[0, spans + 2 + s] for s in two]
     count = [p[s] - lo[s] + 1 for s in two]
@@ -88,14 +85,6 @@
     ]
     for copy in taken:
         copy.start()
-    zbuf[...] = jnp.zeros_like(zbuf)
-
-    def zero_copy(i):
-        return pltpu.make_async_copy(zbuf, dkv_hbm.at[pl.ds(i * zrows, zrows)], zsem.at[i])
-
-    for i in range(zcount):
-        zero_copy(i).start()
-
     for copy in taken:
         copy.wait()
     lane = lax.broadcasted_iota(jnp.int32, (1, NQ), 1)
@@ -182,9 +171,6 @@
         other = lo[s] + i - lo[1 - s]
         return other, (other >= 0) & (other < count[1 - s])
 
-    for i in range(zcount):
-        zero_copy(i).wait()
-
     @pl.loop(0, count[0])
     def _(i):
         other, both = shared(0, i)
@@ -224,20 +210,20 @@
     dq_out.wait()
 
 
-def window_grads(meta, fmeta, qs, gs, qt, gt, kv_all):
+def window_grads(meta, fmeta, qs, gs, qt, gt, kv_all, blank):
     tokens = kv_all.shape[0]
     spans = tokens // SPAN
     wmax = MOST_DOC // SPAN + 1
     wmax = -(-wmax // CH) * CH
     anyspace = pl.BlockSpec(memory_space=pl.ANY)
-    zrows = 1024
     return pl.pallas_call(
         functools.partial(window_kernel, spans=spans),
         out_shape=(
             jax.ShapeDtypeStruct((2 * SPAN, HEADS * HD), jnp.bfloat16),
             jax.ShapeDtypeStruct((tokens, 2 * HD), jnp.bfloat16),
         ),
-        in_specs=[pl.BlockSpec(memory_space=pltpu.SMEM)] + [anyspace] * 7,
+        in_specs=[pl.BlockSpec(memory_space=pltpu.SMEM)] + [anyspace] * 8,
+        input_output_aliases={8: 1},
         out_specs=(anyspace, anyspace),
         scratch_shapes=[pltpu.VMEM(v.shape, v.dtype) for v in (meta, fmeta, qs, gs, qt, gt)]
         + [
@@ -247,15 +233,13 @@
             pltpu.VMEM((HD, NQ), jnp.float32),
             *[pltpu.VMEM((CH * SPAN, NQ), jnp.float32)] * 4,
             *[pltpu.VMEM((CH * SPAN, NQ), jnp.bfloat16)] * 4,
-            pltpu.VMEM((zrows, 2 * HD), jnp.bfloat16),
             pltpu.VMEM((NQ, HD), jnp.float32),
             pltpu.SemaphoreType.DMA((2, wmax)),
-            pltpu.SemaphoreType.DMA((tokens // zrows,)),
             pltpu.SemaphoreType.DMA((2, wmax)),
             pltpu.SemaphoreType.DMA((7,)),
         ],
         name="window_grads",
-    )(meta, meta, fmeta, qs, gs, qt, gt, kv_all)
+    )(meta, meta, fmeta, qs, gs, qt, gt, kv_all, blank)
 
 
 def prepare(q_ref, og_ref, ao_ref, lse_ref, doc_ref, order_ref, qs, gs, qt, gt, meta, fmeta, tmp):
@@ -375,13 +359,18 @@
     return partner
 
 
-GATHER_COPIES = 3 * (3 + 3 + 16 + 16)
+GATHER_COPIES = 3 * (3 + 4 + 16 + 16)
 
 
 def gather_kernel(kv_ref, *refs):
-    sources, targets, out = refs[:6], refs[6:12], refs[12]
-    held, made = refs[13:19], refs[19:25]
-    tmp, send_sem, recv_sem, own_sem, small_sem = refs[25:]
+    sources, targets, out, blank = refs[:6], refs[6:12], refs[12], refs[13]
+    held, made = refs[14:20], refs[20:26]
+    tmp, zeros, send_sem, recv_sem, own_sem, small_sem, zero_sem = refs[26:]
+    zrows = zeros.shape[0]
+    wiped = [
+        pltpu.make_async_copy(zeros, blank.at[pl.ds(k * zrows, zrows)], zero_sem.at[k])
+        for k in range(blank.shape[0] // zrows)
+    ]
     taken = [
         pltpu.make_async_copy(sources[k], held[k], small_sem.at[k]) for k in range(6)
     ]
@@ -441,6 +430,9 @@
     prepare(*held, *made, tmp)
     for copy in given:
         copy.start()
+    zeros[...] = jnp.zeros_like(zeros)
+    for copy in wiped:
+        copy.start()
     own.wait()
     line = [dict(mine, **{ORDERS[i][0]: None}) for i in colors]
     plane = []
@@ -452,17 +444,28 @@
 
     for i in colors:
         settle(first[i])
-        plane.append({d: push(i, line[i], ORDERS[i][1], d) for d in (2, 1, -1)})
+        plane.append(both(i, line[i], ORDERS[i][1]))
     for i in colors:
         wave[i][0] = both(i, piece(i, 0), ORDERS[i][2])
     for i in colors:
         cross(i, line[i])
-    for by in (1, -1, 2):
+    turn = [{} for i in colors]
+    for by in (1, -1):
         for i in colors:
-            plane[i][by if by == 2 else -by].wait_recv()
+            a2 = ORDERS[i][1]
+            plane[i][-by].wait_recv()
+            turn[i][-by] = push(i, piece(i, by), a2, -by, HALF[-by])
+    for by in (1, -1):
+        for i in colors:
             wave[i][by] = both(i, piece(i, by), ORDERS[i][2])
             cross(i, piece(i, by))
-    for by in (0, 1, -1, 2):
+    last0 = [relay(i, piece(i, 0), ORDERS[i][2], wave[i][0]) for i in colors]
+    for i in colors:
+        last[i][0] = last0[i]
+        settle(turn[i])
+        wave[i][2] = both(i, piece(i, 2), ORDERS[i][2])
+        cross(i, piece(i, 2))
+    for by in (1, -1, 2):
         for i in colors:
             last[i][by] = relay(i, piece(i, by), ORDERS[i][2], wave[i][by])
     for by in (0, 1, -1, 2):
@@ -472,7 +475,7 @@
             cross(i, dict(piece(i, by), **{a3: moved(me, a3, 2)[a3]}))
     for copy in across:
         copy.wait_recv()
-    for copy in given:
+    for copy in given + wiped:
         copy.wait()
     net.drain()
 
@@ -497,28 +500,31 @@
         ((8, 2 * span_order.shape[0]), jnp.int32),
         ((8, NQ), jnp.float32),
     ]
-    *small, out = pl.pallas_call(
+    *small, out, blank = pl.pallas_call(
         gather_kernel,
         out_shape=(
             *[jax.ShapeDtypeStruct(*m) for m in made],
             jax.ShapeDtypeStruct((2, 4, 4, 4, rows, COLS), keys_values.dtype),
+            jax.ShapeDtypeStruct((128 * rows, COLS), jnp.bfloat16),
         ),
         in_specs=[vmem] + [anyspace] * 6,
-        out_specs=[anyspace] * 7,
+        out_specs=[anyspace] * 8,
         scratch_shapes=[pltpu.VMEM(v.shape, v.dtype) for v in sources]
         + [pltpu.VMEM(*m) for m in made]
         + [
             pltpu.VMEM((NQ, HD), jnp.float32),
+            pltpu.VMEM((1024, COLS), jnp.bfloat16),
             pltpu.SemaphoreType.DMA((GATHER_COPIES,)),
             pltpu.SemaphoreType.DMA((GATHER_COPIES,)),
             pltpu.SemaphoreType.DMA,
             pltpu.SemaphoreType.DMA((12,)),
+            pltpu.SemaphoreType.DMA((128 * rows // 1024,)),
         ],
         compiler_params=pltpu.CompilerParams(collective_id=0, has_side_effects=True),
         name="gather_keys",
     )(keys_values, *sources)
     qs, gs, qt, gt, meta, fmeta = small
-    return meta, fmeta, qs, gs, qt, gt, out.reshape(128 * rows, COLS)
+    return meta, fmeta, qs, gs, qt, gt, out.reshape(128 * rows, COLS), blank
 
 
 KEYS = (2, 1, -1, 0)
@@ -526,7 +532,7 @@
 
 
 class Scatter:
-    def __init__(self, me, net, mine, other, halves, third, second, first, rows):
+    def __init__(self, me, net, mine, other, third, second, first, halves, rows):
         self.me, self.net, self.mine, self.other, self.halves = me, net, mine, other, halves
         self.buffers = {3: third, 2: second, 1: first}
         self.parts = row_parts(rows)
@@ -552,7 +558,7 @@
         return [((v,), dict(sel, **{ORDERS[i][0]: v})) for v in range(4)]
 
     def lead(self, level, i, key, d):
-        side = AWAY.index(d) if self.halves is None or level < 3 else (0 if d == 1 else 1)
+        side = AWAY.index(d)
         return (i, KEYS.index(key), side) if level == 3 else (i, side)
 
     def slot(self, buf, level, i, key, d):
@@ -574,31 +580,35 @@
             ix = self.ix(i, sel)
             self.mine[ix] = self.mine[ix] + self.other[ix]
 
+    def part_ways(self, level, i, key):
+        sel = self.level_sel(level, i, key, 2)
+        for d in (1, -1):
+            dst = self.slot(self.halves[level], level, i, key, d)
+            src = self.mine.at[self.ix(i, sel, HALF[d])]
+            to = moved(self.me, ORDERS[i][level - 1], d)
+            self.flight["half", level, i, key, d] = self.net.send(src, dst, to)
+
+    def join(self, level, i, key, d):
+        self.flight["half", level, i, key, d].wait_recv()
+        for v, sel in self.blocks(level, i, key, d):
+            ix = self.ix(i, sel, HALF[d])
+            self.mine[ix] = self.mine[ix] + self.halves[level][self.row(level, i, key, d, v)]
+        self.send(level, i, key, d)
+
     def open(self, i, key):
-        if self.halves is None:
+        if 3 not in self.halves:
             for d in AWAY:
                 self.send(3, i, key, d)
             return
-        self.add_core(i, key, 2)
-        sel = self.level_sel(3, i, key, 2)
-        for d in (1, -1):
-            dst = self.slot(self.halves, 3, i, key, d)
-            src = self.mine.at[self.ix(i, sel, HALF[d])]
-            to = moved(self.me, ORDERS[i][2], d)
-            self.flight["half", i, key, d] = self.net.send(src, dst, to)
-        self.add_core(i, key, 1)
-        self.add_core(i, key, -1)
-
-    def turn(self, i, key):
-        for d in (1, -1):
-            self.flight["half", i, key, d].wait_recv()
-            for v, sel in self.blocks(3, i, key, d):
-                ix = self.ix(i, sel, HALF[d])
-                self.mine[ix] = self.mine[ix] + self.halves[self.row(3, i, key, d, v)]
-            self.send(3, i, key, d)
+        if self.other is not None:
+            self.add_core(i, key, 2)
+        self.part_ways(3, i, key)
+        if self.other is not None:
+            self.add_core(i, key, 1)
+            self.add_core(i, key, -1)
 
     def close(self, level, i, key=0, write=None):
-        sides = (1, -1) if level == 3 and self.halves is not None else AWAY
+        sides = (1, -1) if level in self.halves else AWAY
         if level == 3 and self.other is not None:
             self.arrived(i, key, 0)
         for d in sides:
@@ -617,12 +627,18 @@
 
     def finish(self, i, key):
         self.close(3, i, key)
-        if key != 0:
+        if key == 0:
+            return
+        if 2 not in self.halves:
             self.send(2, i, 0, key)
+        elif key == 2:
+            self.part_ways(2, i, 0)
+        else:
+            self.join(2, i, 0, key)
 
     def run(self, ready, write, aside):
         colors = range(3)
-        lag = 1 if self.halves is None else 2
+        lag = 2 if 3 in self.halves else 1
         for n in range(len(KEYS) + lag):
             if n < len(KEYS):
                 for i in colors:
@@ -630,7 +646,8 @@
                     self.open(i, KEYS[n])
             if lag == 2 and 1 <= n <= len(KEYS):
                 for i in colors:
-                    self.turn(i, KEYS[n - 1])
+                    for d in (1, -1):
+                        self.join(3, i, KEYS[n - 1], d)
             if n == len(KEYS) - 1:
                 aside()
             if n >= lag:
@@ -644,30 +661,40 @@
             self.close(1, i, write=write)
 
 
-def scatter_scratch(rows, relayed):
+def scatter_scratch(rows, planes, relayed):
     top = row_parts(rows)[0][1]
-    plane = pltpu.VMEM((4, 4, 4, rows, COLS), jnp.bfloat16)
-    return ([plane, plane, pltpu.VMEM((3, 4, 2, 4, top, HD), jnp.bfloat16)] if relayed else [plane]) + [
-        pltpu.VMEM((3, 4, 2 if relayed else 3, 4, top, COLS), jnp.bfloat16),
-        pltpu.VMEM((3, 3, 4, top, COLS), jnp.bfloat16),
-        pltpu.VMEM((3, 3, top, COLS), jnp.bfloat16),
-    ]
-
-
-SCATTER_COPIES = 3 * (4 * 4 + 3 + 3) + 3 * (4 * 3 + 3 + 3) + 21 + 8 + 1
+    return (
+        [pltpu.VMEM((4, 4, 4, rows, COLS), jnp.bfloat16)] * planes
+        + [
+            pltpu.VMEM((3, 4, 3, 4, top, COLS), jnp.bfloat16),
+            pltpu.VMEM((3, 3, 4, top, COLS), jnp.bfloat16),
+            pltpu.VMEM((3, 3, top, COLS), jnp.bfloat16),
+        ]
+        + [
+            pltpu.VMEM((3, 4, 3, 4, top, HD) if level == 3 else (3, 3, 4, top, HD), jnp.bfloat16)
+            for level in relayed
+        ]
+    )
+
+
+KV_RELAYED = (3, 2)
+W_RELAYED = ()
+SCATTER_COPIES = 2 * 3 * (4 * 4 + 4 + 3) + 21 + 8 + 1
 
 
 def scatter_kernel(part_ref, x_ref, kv_out, w_out, *scratch):
-    kv_bufs, w_bufs = scratch[:6], scratch[6:10]
-    x_buf, x_theirs, xt, pair, send_sem, recv_sem, load_sem = scratch[10:]
+    kv_end = 5 + len(KV_RELAYED)
+    w_end = kv_end + 4 + len(W_RELAYED)
+    kv_bufs, w_bufs = scratch[:kv_end], scratch[kv_end:w_end]
+    x_buf, x_theirs, xt, pair, send_sem, recv_sem, load_sem = scratch[w_end:]
     x_load = pltpu.make_async_copy(x_ref, x_buf, load_sem.at[12])
     me = here()
     core = me["core"]
     rows, w_rows = kv_out.shape[0], w_out.shape[0]
     wide = 8 * w_rows
     net = Copies(send_sem, recv_sem)
-    job = Scatter(me, net, *kv_bufs, rows)
-    w_job = Scatter(me, net, w_bufs[0], None, None, *w_bufs[1:], w_rows)
+    job = Scatter(me, net, *kv_bufs[:5], dict(zip(KV_RELAYED, kv_bufs[5:])), rows)
+    w_job = Scatter(me, net, w_bufs[0], None, *w_bufs[1:4], dict(zip(W_RELAYED, w_bufs[4:])), w_rows)
     loads, swaps = {}, {}
     for n, key in enumerate(KEYS):
         for i in range(3):
@@ -745,8 +772,8 @@
         ),
         in_specs=[pl.BlockSpec(memory_space=pl.ANY)] * 2,
         out_specs=(vmem, vmem),
-        scratch_shapes=scatter_scratch(rows, True)
-        + scatter_scratch(w_rows, False)
+        scratch_shapes=scatter_scratch(rows, 2, KV_RELAYED)
+        + scatter_scratch(w_rows, 1, W_RELAYED)
         + [
             pltpu.VMEM((rows, width), jnp.bfloat16),
             pltpu.VMEM((8, rows, 8 * w_rows), jnp.bfloat16),

time: 101 us -> 99.3 us (0.983)
  Pallas kernels: 99.7 us -> 98.5 us
    pallas_call x1, Pallas kernels: 12.7 us -> 7.05 us  [window_grads(): pl.pallas_call(functools.partial(window_kernel, spans=spans), out_shape=(...]
    pallas_call x1, Pallas kernels: 50.8 us -> 55.3 us  [scatter_grads(): pl.pallas_call(scatter_kernel, out_shape=(jax.ShapeDtypeStruct((rows, COL...]
where the time goes in v8:
time: 99.3 us; the launch traced here: 99.2 us
  Pallas kernels  98.5 us (99%)
    pallas_call x1, Pallas kernels, scatter_grads(): pl.pallas_call(scatter_kernel, out_shape=(jax.ShapeDtypeStruct((rows, COL...  55.3 us
    pallas_call x1, Pallas kernels, gather_keys(): pl.pallas_call(gather_kernel, out_shape=(*[jax.ShapeDtypeStruct(*m) for m...  34.6 us
    pallas_call x1, Pallas kernels, window_grads(): pl.pallas_call(functools.partial(window_kernel, spans=spans), out_shape=(...  7.05 us

profile of v8, /device:TPU:0, one launch (start us, length us, event | category | flops | bytes accessed | tf_op | source)
XLA Modules:
  0.0 99.2 jit_solution(8108634748758900526)
XLA Ops:
  0.6 34.6 %gather_keys.1 = (bf16[2,384,128]{2,1,0:T(8,128)(2,1)}, bf16[2,384,128]{2,1,0:T(8,128)(2,1)}, bf16[2,128,384]{2,1,0:T(8,128)(2,1)}, bf16[2,128,384]{2,1,0:T(8,12...) custom-call(bf16[128,256]{1,0:T(8,128)(2,1)} %kv_ref.1, ...), custom_call_target="tpu_custom_call" | custom-call | tf_op jit(solution)/shard_map/gather_keys/pallas_call | solution.py:503
  35.3 7.0 %window_grads.1 = (bf16[128,768]{1,0:T(8,128)(2,1)}, bf16[16384,256]{1,0:T(8,128)(2,1)}) custom-call(s32[8,512]{1,0:T(8,128)} %get-tuple-element.17.tab.meta_hbm, s32[8,512]{1,0:T(8,128)} %get-tuple-element.17.tab.meta_hbm, f32[8,384]{1,0:T(8,128)} %get-tuple-element.18.fmeta_hbm, ...), custom_call_target="tpu_custom_call", output_to_operand_aliasing={{1}: (8, {})} | custom-call | tf_op jit(solution)/shard_map/window_grads/pallas_call | solution.py:219
  42.3 55.3 %scatter_grads.1 = (bf16[128,256]{1,0:T(8,128)(2,1)}, f32[48,256]{1,0:T(8,128)}) custom-call(bf16[2,4,4,4,128,256]{5,4,3,2,1,0:T(8,128)(2,1)} %bitcast.4, bf16[128,6144]{1,0:T(8,128)(2,1)} %x_ref.1), custom_call_target="tpu_custom_call" | custom-call | tf_op jit(solution)/shard_map/scatter_grads/pallas_call | solution.py:767
  97.7 1.5 %handed_on.1 = (bf16[128,256]{1,0:T(8,128)(2,1)}, f32[48,256]{1,0:T(8,128)}) custom-call(bf16[128,256]{1,0:T(8,128)(2,1)} %get-tuple-element.27.a, f32[48,256]{1,0:T(8,128)} %get-tuple-element.28.b), custom_call_target="tpu_custom_call" | custom-call | tf_op jit(solution)/shard_map/handed_on/pallas_call | solution.py:798

commit v9 on v8

--- a/solution.py
+++ b/solution.py
@@ -110,7 +110,7 @@
             dp[s][...] = jnp.dot(kbuf[s][at, HD:], gt[s], preferred_element_type=jnp.float32)
 
     def weigh(j, two=two):
-        part = 16
+        part = 32
         row = lax.broadcasted_iota(jnp.int32, (part, NQ), 0)
         for n in range(CH * SPAN // part):
             some = slice(n * part, (n + 1) * part)
@@ -528,7 +528,7 @@
 
 
 KEYS = (2, 1, -1, 0)
-AWAY = (2, 1, -1)
+AWAY = (1, -1, 2)
 
 
 class Scatter:

time: 99.3 us -> 99.2 us (level)
  Pallas kernels: 98.5 us -> 97.5 us
    pallas_call x1, Pallas kernels: 55.3 us -> 50.6 us  [scatter_grads(): pl.pallas_call(scatter_kernel, out_shape=(jax.ShapeDtypeStruct((rows, COL...]
    pallas_call x1, Pallas kernels: 7.05 us -> 10.7 us  [window_grads(): pl.pallas_call(functools.partial(window_kernel, spans=spans), out_shape=(...]
where the time goes in v9:
time: 99.2 us; the launch traced here: 98.2 us
  Pallas kernels  97.5 us (98%)
    pallas_call x1, Pallas kernels, scatter_grads(): pl.pallas_call(scatter_kernel, out_shape=(jax.ShapeDtypeStruct((rows, COL...  50.6 us
    pallas_call x1, Pallas kernels, gather_keys(): pl.pallas_call(gather_kernel, out_shape=(*[jax.ShapeDtypeStruct(*m) for m...  34.6 us
    pallas_call x1, Pallas kernels, window_grads(): pl.pallas_call(functools.partial(window_kernel, spans=spans), out_shape=(...  10.7 us

profile of v9, /device:TPU:0, one launch (start us, length us, event | category | flops | bytes accessed | tf_op | source)
XLA Modules:
  0.0 98.2 jit_solution(18437323130589365764)
XLA Ops:
  0.6 34.6 %gather_keys.1 = (bf16[2,384,128]{2,1,0:T(8,128)(2,1)}, bf16[2,384,128]{2,1,0:T(8,128)(2,1)}, bf16[2,128,384]{2,1,0:T(8,128)(2,1)}, bf16[2,128,384]{2,1,0:T(8,12...) custom-call(bf16[128,256]{1,0:T(8,128)(2,1)} %kv_ref.1, ...), custom_call_target="tpu_custom_call" | custom-call | tf_op jit(solution)/shard_map/gather_keys/pallas_call | solution.py:503
  35.3 10.7 %window_grads.1 = (bf16[128,768]{1,0:T(8,128)(2,1)}, bf16[16384,256]{1,0:T(8,128)(2,1)}) custom-call(s32[8,512]{1,0:T(8,128)} %get-tuple-element.17.tab.meta_hbm, s32[8,512]{1,0:T(8,128)} %get-tuple-element.17.tab.meta_hbm, f32[8,384]{1,0:T(8,128)} %get-tuple-element.18.fmeta_hbm, ...), custom_call_target="tpu_custom_call", output_to_operand_aliasing={{1}: (8, {})} | custom-call | tf_op jit(solution)/shard_map/window_grads/pallas_call | solution.py:219
  46.0 50.6 %scatter_grads.1 = (bf16[128,256]{1,0:T(8,128)(2,1)}, f32[48,256]{1,0:T(8,128)}) custom-call(bf16[2,4,4,4,128,256]{5,4,3,2,1,0:T(8,128)(2,1)} %bitcast.4, bf16[128,6144]{1,0:T(8,128)(2,1)} %x_ref.1), custom_call_target="tpu_custom_call" | custom-call | tf_op jit(solution)/shard_map/scatter_grads/pallas_call | solution.py:767
  96.7 1.5 %handed_on.1 = (bf16[128,256]{1,0:T(8,128)(2,1)}, f32[48,256]{1,0:T(8,128)}) custom-call(bf16[128,256]{1,0:T(8,128)(2,1)} %get-tuple-element.27.a, f32[48,256]{1,0:T(8,128)} %get-tuple-element.28.b), custom_call_target="tpu_custom_call" | custom-call | tf_op jit(solution)/shard_map/handed_on/pallas_call | solution.py:798
